TPU v7x, 256 devices: a whole 4x4x8 slice. The times are simulated.
256 devices in a mesh: date: 64 (over z, x, core), space: 4 (over y).
Axes of the slice: x: 4, y: 4, z: 8, core: 2. Of those that a mesh axis runs over, the one named last changes fastest.
Arguments:
- slc: bfloat16 [2, 256, 256, 2048], P(None, 'date', 'space'), may hold values from -6 to 6
- pairs: int32 [384, 2], P('date'), may hold values from 0 to 255, as said below
Outputs:
- coherence: float32 [384, 64, 128], P('date', 'space')
- filtered: float32 [2, 384, 64, 128], P(None, 'date', 'space')
Inputs may be any that keep to these rules, and one draw needn't show every extreme that they name: Pairs of rows k * 6 to (k + 1) * 6 - 1 have their reference date among dates k * 4 to (k + 1) * 4 - 1 and a later secondary date below (k + 2) * 4, and below 256; the pairs of one such block are distinct.
All inputs are finite; a program needn't handle non-finite values.
Results may differ from a plain program's by a relative error of at most 0.0003.
Values may be sent and summed in bfloat16 or wider, within the bound.
No kernel may reach another device: no remote copies, remote signals or barrier semaphores. Data moves between devices by JAX's collectives and lax.ppermute only.
A program may use at most 128 MiB of HBM per device.

v0:
```python
import functools

import jax
import jax.numpy as jnp
import numpy as np
from jax import lax
from jax.experimental import pallas as pl
from jax.experimental.pallas import tpu as pltpu
from jax.sharding import PartitionSpec as P

F32, BF16 = jnp.float32, jnp.bfloat16
PATCHES = 9
LANES = 384


def split(value):
    high = value.astype(BF16)
    return high, (value - high.astype(F32)).astype(BF16)


def split_table(table):
    high = table.astype(np.float32).astype(jnp.bfloat16)
    low = (table - high.astype(np.float64)).astype(np.float32).astype(jnp.bfloat16)
    return high, low


@functools.cache
def filter_tables():
    index = np.arange(32)
    phase = 2.0 * np.pi * np.outer(index, index) / 32.0
    cosine, sine = np.cos(phase), np.sin(phase)
    taper = np.where(index < 16, (index + 0.5) / 16.0, (31.5 - index) / 16.0)
    rows = np.zeros((2, 2, 32, 2, 48))
    for j in range(2):
        at = slice(16 * j, 16 * j + 32)
        rows[0, j, :, 0, at], rows[0, j, :, 1, at] = cosine, sine
        rows[1, j, :, 0, at], rows[1, j, :, 1, at] = -sine, cosine
    rows = rows.reshape(128, 96)
    columns = np.zeros((2, 128, 2, LANES))
    back = np.zeros((2, LANES, 2, 128))
    for c in range(PATCHES):
        for b in range(32):
            column = 16 * c - 16 + b
            if not 0 <= column < 128:
                continue
            at = slice(32 * c, 32 * c + 32)
            columns[0, column, 0, at], columns[1, column, 0, at] = cosine[:, b], sine[:, b]
            columns[0, column, 1, at], columns[1, column, 1, at] = -sine[:, b], cosine[:, b]
            scale = taper[b] / 32.0
            back[0, at, 0, column], back[1, at, 0, column] = cosine[:, b] * scale, -sine[:, b] * scale
            back[0, at, 1, column], back[1, at, 1, column] = sine[:, b] * scale, cosine[:, b] * scale
    columns = columns.reshape(256, 2 * LANES)
    back = back.reshape(2 * LANES, 256)
    final = np.zeros((2, 16, 2, 2, 32))
    for j in range(2):
        for row in range(16):
            a = row + 16 * (1 - j)
            scale = taper[a] / 32.0
            final[0, row, 0, j], final[0, row, 1, j] = cosine[:, a] * scale, -sine[:, a] * scale
            final[1, row, 0, j], final[1, row, 1, j] = sine[:, a] * scale, cosine[:, a] * scale
    final = final.reshape(32, 128)
    rows_high, rows_low = split_table(rows)
    final_high, final_low = split_table(final)
    return (
        np.concatenate([rows_high, rows_high, rows_low], axis=1),
        *split_table(columns),
        *split_table(back),
        np.concatenate([final_high, final_high, final_low], axis=1),
    )


def looks_kernel(pairs_ref, own_ref, next_ref, gamma_ref, coherence_ref, images, terms, total, power):
    chunks = own_ref.shape[-1] // 256
    count = pairs_ref.shape[0]
    half = terms.shape[1] // 2
    for c in range(chunks):
        slot = c % 2
        for date in range(4):
            for part in range(2):
                for side in range(2):
                    at = pl.ds(256 * c + 128 * side, 128)
                    images[slot, date, part, side] = own_ref[part, date, :, at].astype(F32)
                    images[slot, 4 + date, part, side] = next_ref[part, date, :, at].astype(F32)

        def load(date, part, side, phase):
            return images[slot, date, part, side, pl.ds(phase, 16, stride=4), :]

        def keep(index, side, value):
            high, low = split(value)
            at = pl.ds(128 * side, 128)
            terms[slot, pl.ds(16 * index, 16), at] = high
            terms[slot, pl.ds(half + 16 * index, 16), at] = low

        for p in range(count):
            first, second = pairs_ref[p, 0], pairs_ref[p, 1]
            for side in range(2):
                re = im = None
                for phase in range(4):
                    ar, ai = load(first, 0, side, phase), load(first, 1, side, phase)
                    br, bi = load(second, 0, side, phase), load(second, 1, side, phase)
                    one, other = ar * br + ai * bi, ai * br - ar * bi
                    re, im = (one, other) if re is None else (re + one, im + other)
                keep(p, side, re)
                keep(count + p, side, im)
        for date in range(8):
            for side in range(2):
                square = None
                for phase in range(4):
                    re, im = load(date, 0, side, phase), load(date, 1, side, phase)
                    one = re * re + im * im
                    square = one if square is None else square + one
                keep(2 * count + date, side, square)
        sample = lax.broadcasted_iota(jnp.int32, (256, 128), 0)
        column = lax.broadcasted_iota(jnp.int32, (256, 128), 1)
        pool = ((sample >> 4) + 16 * c == column).astype(F32).astype(BF16)
        part = jnp.dot(terms[slot], pool, preferred_element_type=F32)
        total[...] = part if c == 0 else total[...] + part
    power[...] = (
        total[pl.ds(32 * count, 128)] + total[pl.ds(half + 32 * count, 128)]
    ).reshape(8, 16, 128) * (1.0 / 64.0)
    for p in range(count):
        first, second = pairs_ref[p, 0], pairs_ref[p, 1]
        scale = lax.rsqrt((power[first] + 1e-6) * (power[second] + 1e-6)) * (1.0 / 64.0)
        re = (total[pl.ds(16 * p, 16)] + total[pl.ds(half + 16 * p, 16)]) * scale
        at = 16 * (count + p)
        im = (total[pl.ds(at, 16)] + total[pl.ds(half + at, 16)]) * scale
        gamma_ref[0, p] = re
        gamma_ref[1, p] = im
        coherence_ref[p] = jnp.sqrt(re * re + im * im)


def looks(pairs, own, following):
    count = pairs.shape[0]
    rows = 16 * (2 * count + 8)
    vmem = pl.BlockSpec(memory_space=pltpu.VMEM)
    return pl.pallas_call(
        looks_kernel,
        out_shape=(
            jax.ShapeDtypeStruct((2, count, 16, 128), F32),
            jax.ShapeDtypeStruct((count, 16, 128), F32),
        ),
        in_specs=[pl.BlockSpec(memory_space=pltpu.SMEM), vmem, vmem],
        out_specs=(vmem, vmem),
        scratch_shapes=[
            pltpu.VMEM((2, 8, 2, 2, 64, 128), F32),
            pltpu.VMEM((2, 2 * rows, 256), BF16),
            pltpu.VMEM((2 * rows, 128), F32),
            pltpu.VMEM((8, 16, 128), F32),
        ],
        compiler_params=pltpu.CompilerParams(vmem_limit_bytes=32 << 20),
        name="looks",
    )(pairs, own, following)


def ring(power, axis, step, index):
    size = power.shape[axis]
    near = pltpu.roll(power, 1 if step > 0 else size - 1, axis)
    wrap = pltpu.roll(power, size - 31 if step > 0 else 31, axis)
    return jnp.where(index == (0 if step > 0 else 31), wrap, near)


def filter_kernel(
    low_ref, own_ref, high_ref, rows_ref, columns_high, columns_low, back_high, back_low,
    final_ref, out_ref, field, spectra, weighted, result,
):
    count = own_ref.shape[1]
    for p in range(count):
        lanes = pl.ds(128 * p, 128)
        for part in range(2):
            for k, ref in enumerate((low_ref, own_ref, high_ref)):
                high, low = split(ref[part, p])
                at = 48 * part + 16 * k
                field[pl.ds(at, 16), lanes] = high
                field[pl.ds(96 + at, 16), lanes] = low
                field[pl.ds(192 + at, 16), lanes] = high
    along = jnp.dot(rows_ref[...], field[...], preferred_element_type=F32)
    for p in range(count):
        for part in range(2):
            high, low = split(along[64 * part : 64 * part + 64, 128 * p : 128 * p + 128])
            spectra[0, pl.ds(64 * p, 64), pl.ds(128 * part, 128)] = high
            spectra[1, pl.ds(64 * p, 64), pl.ds(128 * part, 128)] = low
    lane = lax.broadcasted_iota(jnp.int32, (64, 128), 1) & 31
    line = lax.broadcasted_iota(jnp.int32, (64, 128), 0) & 31
    for block in range(LANES // 128):
        parts = []
        for part in range(2):
            at = pl.ds(LANES * part + 128 * block, 128)
            parts.append(
                jnp.dot(spectra[0], columns_high[:, at], preferred_element_type=F32)
                + jnp.dot(spectra[1], columns_high[:, at], preferred_element_type=F32)
                + jnp.dot(spectra[0], columns_low[:, at], preferred_element_type=F32)
            )
        for p in range(count):
            re, im = (value[64 * p : 64 * p + 64] for value in parts)
            power = re * re + im * im
            power = power + ring(power, 1, 1, lane) + ring(power, 1, -1, lane)
            power = power + ring(power, 0, 1, line) + ring(power, 0, -1, line)
            weight = lax.rsqrt(lax.rsqrt(power * (1.0 / 9.0) + 1e-6))
            for part, value in enumerate((re, im)):
                high, low = split(value * weight)
                at = pl.ds(LANES * part + 128 * block, 128)
                weighted[0, pl.ds(64 * p, 64), at] = high
                weighted[1, pl.ds(64 * p, 64), at] = low
    across = (
        jnp.dot(weighted[0], back_high[...], preferred_element_type=F32)
        + jnp.dot(weighted[1], back_high[...], preferred_element_type=F32)
        + jnp.dot(weighted[0], back_low[...], preferred_element_type=F32)
    )
    for p in range(count):
        lanes = pl.ds(128 * p, 128)
        for part in range(2):
            high, low = split(across[64 * p : 64 * p + 64, 128 * part : 128 * part + 128])
            at = 64 * part
            result[pl.ds(at, 64), lanes] = high
            result[pl.ds(128 + at, 64), lanes] = low
            result[pl.ds(256 + at, 64), lanes] = high
    out = jnp.dot(final_ref[...], result[...], preferred_element_type=F32)
    for p in range(count):
        for part in range(2):
            out_ref[part, p] = out[16 * part : 16 * part + 16, 128 * p : 128 * p + 128]


def goldstein(low, own, high):
    count = own.shape[1]
    vmem = pl.BlockSpec(memory_space=pltpu.VMEM)
    tables = [jnp.asarray(table) for table in filter_tables()]
    return pl.pallas_call(
        filter_kernel,
        out_shape=jax.ShapeDtypeStruct((2, count, 16, 128), F32),
        in_specs=[vmem] * 9,
        out_specs=vmem,
        scratch_shapes=[
            pltpu.VMEM((288, 128 * count), BF16),
            pltpu.VMEM((2, 64 * count, 256), BF16),
            pltpu.VMEM((2, 64 * count, 2 * LANES), BF16),
            pltpu.VMEM((384, 128 * count), BF16),
        ],
        compiler_params=pltpu.CompilerParams(vmem_limit_bytes=32 << 20),
        name="goldstein",
    )(low, own, high, *tables)


def per_device(slc, pairs):
    dates = lax.axis_size("date")
    strips = lax.axis_size("space")
    local_pairs = pairs - lax.axis_index("date") * slc.shape[1]
    following = lax.ppermute(slc, "date", [(i + 1, i) for i in range(dates - 1)])
    gamma, coherence = looks(local_pairs, slc, following)
    low = lax.ppermute(gamma, "space", [(i, i + 1) for i in range(strips - 1)])
    high = lax.ppermute(gamma, "space", [(i + 1, i) for i in range(strips - 1)])
    return coherence, goldstein(low, gamma, high)


def solution(mesh):
    return jax.shard_map(
        per_device,
        mesh=mesh,
        in_specs=(P(None, "date", "space", None), P("date", None)),
        out_specs=(P("date", "space", None), P(None, "date", "space", None)),
        check_vma=False,
    )
```

profile of v0, /device:TPU:127, one launch (start us, length us, event | category | flops | bytes accessed | tf_op | source)
XLA Modules:
  0.0 50.1 jit_solution(8867504132731439248)
XLA Ops:
  0.6 2.6 %collective-permute-start = (bf16[2,4,64,2048]{3,2,1,0:T(8,128)(2,1)}, bf16[2,4,64,2048]{3,2,1,0:T(8,128)(2,1)S(1)}, u32[]{:S(2)}, u32[]{:S(2)}) collective-permute-start(bf16[2,4,64,2048]{3,2,1,0:T(8,128)(2,1)} %own_ref.1), channel_id=1, source_target_pairs={{4,0},{8,4},{12,8},{16,12},{20,16},{24,20},{28,24},{32,28},{36,32}... | collective-permute-start | bytes 6291464 | tf_op jit(solution)/shard_map/ppermute | solution.py:247
  3.2 0.8 %copy.10 = s32[6,2]{1,0:T(8,128)S(1)} copy(s32[6,2]{0,1:T(2,128)} %param.9) | data formatting | bytes 96 | tf_op args[1]
  4.0 27.5 %collective-permute-done.next_ref = bf16[2,4,64,2048]{3,2,1,0:T(8,128)(2,1)S(1)} collective-permute-done((bf16[2,4,64,2048]{3,2,1,0:T(8,128)(2,1)}, bf16[2,4,64,2048]{3,2,1,0:T(8,128)(2,1)S(1)}, u32[]{:S(2)}, u32[]{:S(2)}) %collective-permute-start) | collective-permute-done | bytes 2097184 | tf_op jit(solution)/shard_map/ppermute | solution.py:247
  31.5 0.0 copy-start
  31.5 1.6 %copy-done = bf16[2,4,64,2048]{3,2,1,0:T(8,128)(2,1)S(1)} copy-done((bf16[2,4,64,2048]{3,2,1,0:T(8,128)(2,1)S(1)}, bf16[2,4,64,2048]{3,2,1,0:T(8,128)(2,1)}, u32[]{:S(2)}) %copy-start) | copy-done | bytes 2097176
  33.1 0.0 copy-start.1
  33.1 0.0 copy-start.2
  33.1 0.0 copy-start.3
  33.1 0.0 copy-start.4
  33.1 0.0 copy-start.5
  33.1 0.0 copy-start.6
  33.1 5.6 %looks.1 = (f32[2,6,16,128]{3,2,1,0:T(8,128)S(1)}, f32[6,16,128]{2,1,0:T(8,128)}) custom-call(s32[6,2]{1,0:T(8,128)S(1)} %broadcast_subtract_fusion.pairs_ref, bf16[2,4,64,2048]{3,2,1,0:T(8,128)(2,1)S(1)} %copy-done, bf16[2,4,64,2048]{3,2,1,0:T(8,128)(2,1)S(1)} %collective-permute-done.next_ref), custom_call_target="tpu_custom_call" | custom-call | tf_op jit(solution)/shard_map/looks/pallas_call | solution.py:136
  38.7 2.4 %collective-permute-start.2 = (f32[2,6,16,128]{3,2,1,0:T(8,128)S(1)}, f32[2,6,16,128]{3,2,1,0:T(8,128)S(1)}, u32[]{:S(2)}, u32[]{:S(2)}) collective-permute-start(f32[2,6,16,128]{3,2,1,0:T(8,128)S(1)} %get-tuple-element.5.own_ref), channel_id=1, source_target_pairs={{1,0},{2,1},{3,2},{5,4},{6,5},{7,6},{9,8},{10,9},{11,10},{13,12},{... | collective-permute-start | bytes 294920 | tf_op jit(solution)/shard_map/ppermute | solution.py:250
  41.1 1.3 %collective-permute-start.1 = (f32[2,6,16,128]{3,2,1,0:T(8,128)S(1)}, f32[2,6,16,128]{3,2,1,0:T(8,128)S(1)}, u32[]{:S(2)}, u32[]{:S(2)}) collective-permute-start(f32[2,6,16,128]{3,2,1,0:T(8,128)S(1)} %get-tuple-element.5.own_ref), channel_id=1, source_target_pairs={{0,1},{1,2},{2,3},{4,5},{5,6},{6,7},{8,9},{9,10},{10,11},{12,13},{... | collective-permute-start | bytes 294920 | tf_op jit(solution)/shard_map/ppermute | solution.py:249
  42.4 0.3 collective-permute-done.2.high_ref
  42.7 3.7 %collective-permute-done.1.low_ref = f32[2,6,16,128]{3,2,1,0:T(8,128)S(1)} collective-permute-done((f32[2,6,16,128]{3,2,1,0:T(8,128)S(1)}, f32[2,6,16,128]{3,2,1,0:T(8,128)S(1)}, u32[]{:S(2)}, u32[]{:S(2)}) %collective-permute-start.1) | collective-permute-done | bytes 98336 | tf_op jit(solution)/shard_map/ppermute | solution.py:249
  46.5 0.0 copy-done.1
  46.5 0.0 copy-done.2
  46.5 0.0 copy-done.3
  46.5 0.0 copy-done.4
  46.5 0.0 copy-done.5
  46.5 0.0 copy-done.6
  46.5 3.6 %goldstein.1 = f32[2,6,16,128]{3,2,1,0:T(8,128)} custom-call(f32[2,6,16,128]{3,2,1,0:T(8,128)S(1)} %collective-permute-done.1.low_ref, f32[2,6,16,128]{3,2,1,0:T(8,128)S(1)} %get-tuple-element.5.own_ref, f32[2,6,16,128]{3,2,1,0:T(8,128)S(1)} %collective-permute-done.2.high_ref, bf16[128,288]{1,0:T(8,128)(2,1)S(1)} %copy-done.5, ...), custom_call_target="tpu_custom_call" | custom-call | tf_op jit(solution)/shard_map/goldstein/pallas_call | solution.py:227
  (1 shorter events, 0.0 us)
Async XLA Ops:
  0.6 30.9 %collective-permute-start = (bf16[2,4,64,2048]{3,2,1,0:T(8,128)(2,1)}, bf16[2,4,64,2048]{3,2,1,0:T(8,128)(2,1)S(1)}, u32[]{:S(2)}, u32[]{:S(2)}) collective-permute-start(bf16[2,4,64,2048]{3,2,1,0:T(8,128)(2,1)} %own_ref.1), channel_id=1, source_target_pairs={{4,0},{8,4},{12,8},{16,12},{20,16},{24,20},{28,24},{32,28},{36,32}... | collective-permute-start | bytes 6291464 | tf_op jit(solution)/shard_map/ppermute | solution.py:247
  31.5 1.6 %copy-start = (bf16[2,4,64,2048]{3,2,1,0:T(8,128)(2,1)S(1)}, bf16[2,4,64,2048]{3,2,1,0:T(8,128)(2,1)}, u32[]{:S(2)}) copy-start(bf16[2,4,64,2048]{3,2,1,0:T(8,128)(2,1)} %own_ref.1) | copy-start | bytes 6291460
  33.1 13.4 %copy-start.1 = (bf16[768,256]{1,0:T(8,128)(2,1)S(1)}, bf16[768,256]{1,0:T(8,128)(2,1)}, u32[]{:S(2)}) copy-start(bf16[768,256]{1,0:T(8,128)(2,1)} %constant.24.clone.back_low) | copy-start | bytes 1179652
  33.1 13.4 %copy-start.2 = (bf16[768,256]{1,0:T(8,128)(2,1)S(1)}, bf16[768,256]{1,0:T(8,128)(2,1)}, u32[]{:S(2)}) copy-start(bf16[768,256]{1,0:T(8,128)(2,1)} %constant.23.clone.back_high) | copy-start | bytes 1179652
  33.1 13.4 %copy-start.3 = (bf16[256,768]{1,0:T(8,128)(2,1)S(1)}, bf16[256,768]{1,0:T(8,128)(2,1)}, u32[]{:S(2)}) copy-start(bf16[256,768]{1,0:T(8,128)(2,1)} %constant.22.clone.columns_low) | copy-start | bytes 1179652
  33.1 13.4 %copy-start.4 = (bf16[256,768]{1,0:T(8,128)(2,1)S(1)}, bf16[256,768]{1,0:T(8,128)(2,1)}, u32[]{:S(2)}) copy-start(bf16[256,768]{1,0:T(8,128)(2,1)} %constant.21.clone.columns_high) | copy-start | bytes 1179652
  33.1 13.4 %copy-start.5 = (bf16[128,288]{1,0:T(8,128)(2,1)S(1)}, bf16[128,288]{1,0:T(8,128)(2,1)}, u32[]{:S(2)}) copy-start(bf16[128,288]{1,0:T(8,128)(2,1)} %constant.20.clone.rows_ref) | copy-start | bytes 221188
  33.1 13.4 %copy-start.6 = (bf16[32,384]{1,0:T(8,128)(2,1)S(1)}, bf16[32,384]{1,0:T(8,128)(2,1)}, u32[]{:S(2)}) copy-start(bf16[32,384]{1,0:T(8,128)(2,1)} %constant.25.clone.final_ref) | copy-start | bytes 73732
  38.7 4.0 %collective-permute-start.2 = (f32[2,6,16,128]{3,2,1,0:T(8,128)S(1)}, f32[2,6,16,128]{3,2,1,0:T(8,128)S(1)}, u32[]{:S(2)}, u32[]{:S(2)}) collective-permute-start(f32[2,6,16,128]{3,2,1,0:T(8,128)S(1)} %get-tuple-element.5.own_ref), channel_id=1, source_target_pairs={{1,0},{2,1},{3,2},{5,4},{6,5},{7,6},{9,8},{10,9},{11,10},{13,12},{... | collective-permute-start | bytes 294920 | tf_op jit(solution)/shard_map/ppermute | solution.py:250
  41.1 5.4 %collective-permute-start.1 = (f32[2,6,16,128]{3,2,1,0:T(8,128)S(1)}, f32[2,6,16,128]{3,2,1,0:T(8,128)S(1)}, u32[]{:S(2)}, u32[]{:S(2)}) collective-permute-start(f32[2,6,16,128]{3,2,1,0:T(8,128)S(1)} %get-tuple-element.5.own_ref), channel_id=1, source_target_pairs={{0,1},{1,2},{2,3},{4,5},{5,6},{6,7},{8,9},{9,10},{10,11},{12,13},{... | collective-permute-start | bytes 294920 | tf_op jit(solution)/shard_map/ppermute | solution.py:249
where the time goes:
time: 50.3 us; the launch traced here: 50.1 us
  waiting for transfers between devices  31.6 us (63%)
  Pallas kernels  9.22 us (18%)
  starting transfers between devices  6.24 us (12%)
  local copies, waits for them, and re-layouts  2.39 us (5%)
  between operations  0.71 us (1%)
    ppermute x1, waiting for transfers between devices, per_device(): lax.ppermute(slc, 'date', [(i + 1, i) for i in range(dates - 1)])  27.5 us
    pallas_call x1, Pallas kernels, looks(): pl.pallas_call(looks_kernel, out_shape=(jax.ShapeDtypeStruct((2, count, 1...  5.6 us
    ppermute x1, waiting for transfers between devices, per_device(): low = lax.ppermute(gamma, 'space', [(i, i + 1) for i in range(strips - 1)])  3.74 us
    pallas_call x1, Pallas kernels, goldstein(): pl.pallas_call(filter_kernel, out_shape=jax.ShapeDtypeStruct((2, count, 1...  3.62 us
    ppermute x1, starting transfers between devices, per_device(): lax.ppermute(slc, 'date', [(i + 1, i) for i in range(dates - 1)])  2.59 us
    unnamed x15, local copies, waits for them, and re-layouts  2.39 us
    ppermute x1, starting transfers between devices, per_device(): high = lax.ppermute(gamma, 'space', [(i + 1, i) for i in range(strips - 1)])  2.36 us
    ppermute x1, starting transfers between devices, per_device(): low = lax.ppermute(gamma, 'space', [(i, i + 1) for i in range(strips - 1)])  1.29 us
  transfers between devices with their start and end apart: 3, of which 3 were waited for; matrix products, arithmetic and copies ran while one was open for 2% of the time, Pallas kernels for 0%

commit v1 on v0

v1 whole, which is shorter than its diff:
```python
import functools

import jax
import jax.numpy as jnp
import numpy as np
from jax import lax
from jax.experimental import pallas as pl
from jax.experimental.pallas import tpu as pltpu
from jax.sharding import PartitionSpec as P

F32, BF16 = jnp.float32, jnp.bfloat16
PATCHES, BLOCKS = 9, 3


def split(value):
    high = value.astype(BF16)
    return high, (value - high.astype(F32)).astype(BF16)


def split_table(table):
    high = table.astype(np.float32).astype(jnp.bfloat16)
    low = (table - high.astype(np.float64)).astype(np.float32).astype(jnp.bfloat16)
    return high, low


@functools.cache
def filter_tables():
    index = np.arange(32)
    phase = 2.0 * np.pi * np.outer(index, index) / 32.0
    cosine, sine = np.cos(phase), np.sin(phase)
    taper = np.where(index < 16, (index + 0.5) / 16.0, (31.5 - index) / 16.0)
    rows = np.zeros((2, 2, 32, 2, 48))
    final = np.zeros((2, 16, 2, 2, 32))
    for j in range(2):
        at = slice(16 * j, 16 * j + 32)
        rows[0, j, :, 0, at], rows[0, j, :, 1, at] = cosine, sine
        rows[1, j, :, 0, at], rows[1, j, :, 1, at] = -sine, cosine
        for row in range(16):
            a = row + 16 * (1 - j)
            scale = taper[a] / 32.0
            final[0, row, 0, j], final[0, row, 1, j] = cosine[:, a] * scale, -sine[:, a] * scale
            final[1, row, 0, j], final[1, row, 1, j] = sine[:, a] * scale, cosine[:, a] * scale
    rows_high, rows_low = split_table(rows.reshape(128, 96))
    final_high, final_low = split_table(final.reshape(32, 128))
    lane = np.arange(128)
    place = (np.arange(32)[:, None] + 16 - 16 * (lane // 32)[None]) % 32
    fore = 2.0 * np.pi * place * (lane % 32)[None] / 32.0
    place = (lane[None] + 16 - 16 * (lane // 32)[:, None]) % 32
    back = 2.0 * np.pi * place * (lane % 32)[:, None] / 32.0
    scale = taper[place] / 32.0
    return (
        np.concatenate([rows_high, rows_high, rows_low], axis=1),
        np.concatenate([final_high, final_high, final_low], axis=1),
        np.stack([*split_table(np.cos(fore)), *split_table(np.sin(fore))]),
        np.stack([*split_table(np.cos(back) * scale), *split_table(np.sin(back) * scale)]),
    )


def looks_kernel(pairs_ref, own_ref, next_ref, *refs, start, added, coherence):
    extra, refs = refs[:added], refs[added:]
    gamma_ref, refs = refs[0], refs[1:]
    if coherence:
        coherence_ref, refs = refs[0], refs[1:]
    images, terms, total, power = refs
    chunks = own_ref.shape[-1] // 256
    count = pairs_ref.shape[0]
    half = terms.shape[1] // 2
    for c in range(chunks):
        slot = c % 2
        for date in range(4):
            for part in range(2):
                for side in range(2):
                    at = pl.ds(256 * c + 128 * side, 128)
                    images[slot, date, part, side] = own_ref[part, date, :, at].astype(F32)
                    images[slot, 4 + date, part, side] = next_ref[part, date, :, at].astype(F32)

        def load(date, part, side, phase):
            return images[slot, date, part, side, pl.ds(phase, 16, stride=4), :]

        def keep(index, side, value):
            high, low = split(value)
            at = pl.ds(128 * side, 128)
            terms[slot, pl.ds(16 * index, 16), at] = high
            terms[slot, pl.ds(half + 16 * index, 16), at] = low

        for p in range(count):
            first, second = pairs_ref[p, 0], pairs_ref[p, 1]
            for side in range(2):
                re = im = None
                for phase in range(4):
                    ar, ai = load(first, 0, side, phase), load(first, 1, side, phase)
                    br, bi = load(second, 0, side, phase), load(second, 1, side, phase)
                    one, other = ar * br + ai * bi, ai * br - ar * bi
                    re, im = (one, other) if re is None else (re + one, im + other)
                keep(p, side, re)
                keep(count + p, side, im)
        for date in range(8):
            for side in range(2):
                square = None
                for phase in range(4):
                    re, im = load(date, 0, side, phase), load(date, 1, side, phase)
                    one = re * re + im * im
                    square = one if square is None else square + one
                keep(2 * count + date, side, square)
        sample = lax.broadcasted_iota(jnp.int32, (256, 128), 0)
        column = lax.broadcasted_iota(jnp.int32, (256, 128), 1)
        pool = ((sample >> 4) + (start // 16 + 16 * c) == column).astype(F32).astype(BF16)
        part = jnp.dot(terms[slot], pool, preferred_element_type=F32)
        total[...] = part if c == 0 else total[...] + part
    power[...] = (
        total[pl.ds(32 * count, 128)] + total[pl.ds(half + 32 * count, 128)]
    ).reshape(8, 16, 128) * (1.0 / 64.0)
    for p in range(count):
        first, second = pairs_ref[p, 0], pairs_ref[p, 1]
        scale = lax.rsqrt((power[first] + 1e-6) * (power[second] + 1e-6)) * (1.0 / 64.0)
        re = (total[pl.ds(16 * p, 16)] + total[pl.ds(half + 16 * p, 16)]) * scale
        at = 16 * (count + p)
        im = (total[pl.ds(at, 16)] + total[pl.ds(half + at, 16)]) * scale
        for ref in extra:
            re, im = re + ref[0, p], im + ref[1, p]
        gamma_ref[0, p] = re
        gamma_ref[1, p] = im
        if coherence:
            coherence_ref[p] = jnp.sqrt(re * re + im * im)


def looks(pairs, own, following, start, extra=(), coherence=False, name="looks"):
    count = pairs.shape[0]
    rows = 16 * (2 * count + 8)
    vmem = pl.BlockSpec(memory_space=pltpu.VMEM)
    shapes = [jax.ShapeDtypeStruct((2, count, 16, 128), F32)]
    if coherence:
        shapes.append(jax.ShapeDtypeStruct((count, 16, 128), F32))
    return pl.pallas_call(
        functools.partial(looks_kernel, start=start, added=len(extra), coherence=coherence),
        out_shape=shapes,
        in_specs=[pl.BlockSpec(memory_space=pltpu.SMEM)] + [vmem] * (2 + len(extra)),
        out_specs=[vmem] * len(shapes),
        scratch_shapes=[
            pltpu.VMEM((2, 8, 2, 2, 64, 128), F32),
            pltpu.VMEM((2, 2 * rows, 256), BF16),
            pltpu.VMEM((2 * rows, 128), F32),
            pltpu.VMEM((8, 16, 128), F32),
        ],
        compiler_params=pltpu.CompilerParams(vmem_limit_bytes=12 << 20),
        name=name,
    )(pairs, own, following, *extra)


def ring(power, axis, step, index):
    size = power.shape[axis]
    near = pltpu.roll(power, 1 if step > 0 else size - 1, axis)
    wrap = pltpu.roll(power, size - 31 if step > 0 else 31, axis)
    return jnp.where(index == (0 if step > 0 else 31), wrap, near)


def filter_kernel(
    odd_ref, near_ref, own_ref, far_ref, rows_ref, final_ref, fore_ref, back_ref,
    out_ref, field, spectra, weighted, result, fore, back,
):
    count = own_ref.shape[1]
    odd = 32 * odd_ref[0]
    for p in range(count):
        lanes = pl.ds(128 * p, 128)
        for part in range(2):
            for place, ref in ((32 - odd, near_ref), (16, own_ref), (odd, far_ref)):
                high, low = split(ref[part, p])
                at = pl.multiple_of(48 * part + place, 16)
                field[pl.ds(at, 16), lanes] = high
                field[pl.ds(96 + at, 16), lanes] = low
                field[pl.ds(192 + at, 16), lanes] = high
    across = lax.broadcasted_iota(jnp.int32, (128, 128), 0)
    along = lax.broadcasted_iota(jnp.int32, (128, 128), 1)
    for level in range(2):
        cosine = jnp.concatenate([fore_ref[level].astype(F32)] * 4, axis=0)
        sine = jnp.concatenate([fore_ref[2 + level].astype(F32)] * 4, axis=0)
        for block in range(BLOCKS):
            patch = 4 * block + (along >> 5) - (across >> 4)
            inside = (patch >= 0) & (patch <= 1) & (4 * block + (along >> 5) < PATCHES)
            cos, sin = (jnp.where(inside, value, 0.0) for value in (cosine, sine))
            at = 256 * block
            fore[level, pl.ds(0, 128), pl.ds(at, 128)] = cos.astype(BF16)
            fore[level, pl.ds(128, 128), pl.ds(at, 128)] = sin.astype(BF16)
            fore[level, pl.ds(0, 128), pl.ds(at + 128, 128)] = (-sin).astype(BF16)
            fore[level, pl.ds(128, 128), pl.ds(at + 128, 128)] = cos.astype(BF16)
    column = jnp.dot(rows_ref[...], field[...], preferred_element_type=F32)
    for p in range(count):
        for part in range(2):
            high, low = split(column[64 * part : 64 * part + 64, 128 * p : 128 * p + 128])
            spectra[0, pl.ds(64 * p, 64), pl.ds(128 * part, 128)] = high
            spectra[1, pl.ds(64 * p, 64), pl.ds(128 * part, 128)] = low
    for level in range(2):
        cosine, sine = back_ref[level].astype(F32), back_ref[2 + level].astype(F32)
        for block in range(BLOCKS):
            patch = 4 * block + (across >> 5) - (along >> 4)
            inside = (patch >= 0) & (patch <= 1) & (4 * block + (across >> 5) < PATCHES)
            cos, sin = (jnp.where(inside, value, 0.0) for value in (cosine, sine))
            at = 256 * block
            back[level, pl.ds(at, 128), pl.ds(0, 128)] = cos.astype(BF16)
            back[level, pl.ds(at, 128), pl.ds(128, 128)] = sin.astype(BF16)
            back[level, pl.ds(at + 128, 128), pl.ds(0, 128)] = (-sin).astype(BF16)
            back[level, pl.ds(at + 128, 128), pl.ds(128, 128)] = cos.astype(BF16)
    lane = lax.broadcasted_iota(jnp.int32, (64, 128), 1) & 31
    line = lax.broadcasted_iota(jnp.int32, (64, 128), 0) & 31
    for block in range(BLOCKS):
        at = pl.ds(256 * block, 256)
        both = (
            jnp.dot(spectra[0], fore[0, :, at], preferred_element_type=F32)
            + jnp.dot(spectra[1], fore[0, :, at], preferred_element_type=F32)
            + jnp.dot(spectra[0], fore[1, :, at], preferred_element_type=F32)
        )
        for p in range(count):
            re, im = both[64 * p : 64 * p + 64, :128], both[64 * p : 64 * p + 64, 128:]
            power = re * re + im * im
            power = power + ring(power, 1, 1, lane) + ring(power, 1, -1, lane)
            power = power + ring(power, 0, 1, line) + ring(power, 0, -1, line)
            weight = lax.rsqrt(lax.rsqrt(power * (1.0 / 9.0) + 1e-6))
            for part, value in enumerate((re, im)):
                high, low = split(value * weight)
                at = pl.ds(256 * block + 128 * part, 128)
                weighted[0, pl.ds(64 * p, 64), at] = high
                weighted[1, pl.ds(64 * p, 64), at] = low
    filtered = (
        jnp.dot(weighted[0], back[0], preferred_element_type=F32)
        + jnp.dot(weighted[1], back[0], preferred_element_type=F32)
        + jnp.dot(weighted[0], back[1], preferred_element_type=F32)
    )
    for p in range(count):
        lanes = pl.ds(128 * p, 128)
        for part in range(2):
            high, low = split(filtered[64 * p : 64 * p + 64, 128 * part : 128 * part + 128])
            at = 64 * part
            result[pl.ds(at, 64), lanes] = high
            result[pl.ds(128 + at, 64), lanes] = low
            result[pl.ds(256 + at, 64), lanes] = high
    out = jnp.dot(final_ref[...], result[...], preferred_element_type=F32)
    for p in range(count):
        for part in range(2):
            out_ref[part, p] = out[16 * part : 16 * part + 16, 128 * p : 128 * p + 128]


def goldstein(odd, near, own, far):
    count = own.shape[1]
    vmem = pl.BlockSpec(memory_space=pltpu.VMEM)
    tables = [jnp.asarray(table) for table in filter_tables()]
    return pl.pallas_call(
        filter_kernel,
        out_shape=jax.ShapeDtypeStruct((2, count, 16, 128), F32),
        in_specs=[pl.BlockSpec(memory_space=pltpu.SMEM)] + [vmem] * (3 + len(tables)),
        out_specs=vmem,
        scratch_shapes=[
            pltpu.VMEM((288, 128 * count), BF16),
            pltpu.VMEM((2, 64 * count, 256), BF16),
            pltpu.VMEM((2, 64 * count, 256 * BLOCKS), BF16),
            pltpu.VMEM((384, 128 * count), BF16),
            pltpu.VMEM((2, 256, 256 * BLOCKS), BF16),
            pltpu.VMEM((2, 256 * BLOCKS, 256), BF16),
        ],
        compiler_params=pltpu.CompilerParams(vmem_limit_bytes=16 << 20),
        name="goldstein",
    )(odd, near, own, far, *tables)


def shifted(value, axis, step):
    size = lax.axis_size(axis)
    return lax.ppermute(value, axis, [(i, (i + step) % size) for i in range(size)])


def swapped(value, axis, first):
    size = lax.axis_size(axis)
    pairs = [(i, i + 1) for i in range(first, size - 1, 2)]
    return lax.ppermute(value, axis, pairs + [(j, i) for i, j in pairs])


COLUMNS = (768, 512, 256)


def per_device(slc, pairs):
    dates = slc.shape[1]
    block = lax.axis_index("date")
    here = pairs - block * dates
    edge = sum(COLUMNS)
    own_last = slc[..., edge:]
    previous_last = shifted(own_last, "date", 1)
    own, following, starts, at = [], [], [], 0
    for width in COLUMNS:
        own.append(slc[..., at : at + width])
        following.append(shifted(own[-1], "date", -1))
        starts.append(at)
        at += width
    there = shifted(here, "date", 1)
    [returned] = looks(there, previous_last, own_last, edge, name="looks_last")
    returned = shifted(returned, "date", -1)
    parts = []
    for k in range(len(COLUMNS) - 1):
        parts += looks(here, own[k], following[k], starts[k], name="looks_part")
    gamma, coherence = looks(
        here, own[-1], following[-1], starts[-1], (*parts, returned), True, name="looks_end"
    )
    near = swapped(gamma, "space", 0)
    far = swapped(gamma, "space", 1)
    odd = (lax.axis_index("space") % 2).astype(jnp.int32).reshape(1)
    return coherence, goldstein(odd, near, gamma, far)


def solution(mesh):
    return jax.shard_map(
        per_device,
        mesh=mesh,
        in_specs=(P(None, "date", "space", None), P("date", None)),
        out_specs=(P("date", "space", None), P(None, "date", "space", None)),
        check_vma=False,
    )
```

time: 50.3 us -> 43.1 us (0.86)
  the two profiles are of different devices: /device:TPU:127 before, /device:TPU:16 now
where the time goes in v1:
time: 43.1 us; the launch traced here: 42.9 us
  starting transfers between devices  16.5 us (38%)
  Pallas kernels  11.2 us (26%)
  waiting for transfers between devices  10.8 us (25%)
  local copies, waits for them, and re-layouts  3.58 us (8%)
  between operations  0.82 us (2%)
    ppermute x6, starting transfers between devices, shifted(): lax.ppermute(value, axis, [(i, (i + step) % size) for i in range(size)])  13.4 us
    pallas_call x4, Pallas kernels, looks(): pl.pallas_call(functools.partial(looks_kernel, start=start, added=len(ext...  7.78 us
    ppermute x6, waiting for transfers between devices, shifted(): lax.ppermute(value, axis, [(i, (i + step) % size) for i in range(size)])  5.89 us
    ppermute x2, waiting for transfers between devices, swapped(): return lax.ppermute(value, axis, pairs + [(j, i) for i, j in pairs])  4.87 us
    pallas_call x1, Pallas kernels, goldstein(): pl.pallas_call(filter_kernel, out_shape=jax.ShapeDtypeStruct((2, count, 1...  3.38 us
    ppermute x2, starting transfers between devices, swapped(): return lax.ppermute(value, axis, pairs + [(j, i) for i, j in pairs])  3.19 us
    slice x2, local copies, waits for them, and re-layouts, per_device(): own.append(slc[..., at:at + width])  2.16 us
    slice x1, local copies, waits for them, and re-layouts, per_device(): own_last = slc[..., edge:]  1.29 us
  transfers between devices with their start and end apart: 8, of which 3 were waited for; matrix products, arithmetic and copies ran while one was open for 5% of the time, Pallas kernels for 13%

profile of v1, /device:TPU:16, one launch (start us, length us, event | category | flops | bytes accessed | tf_op | source)
XLA Modules:
  0.0 42.9 jit_solution(12020573772754458625)
XLA Ops:
  0.6 1.2 %slice.13.own_ref = bf16[2,4,64,768]{3,2,1,0:T(8,128)(2,1)S(1)} slice(bf16[2,4,64,2048]{3,2,1,0:T(8,128)(2,1)} %param.6), slice={[0:2], [0:4], [0:64], [0:768]} | slice | bytes 1572864 | tf_op jit(solution)/shard_map/slice | solution.py:287
  1.8 7.6 %collective-permute-start.1 = (bf16[2,4,64,768]{3,2,1,0:T(8,128)(2,1)S(1)}, bf16[2,4,64,768]{3,2,1,0:T(8,128)(2,1)S(1)}, u32[]{:S(2)}, u32[]{:S(2)}) collective-permute-start(bf16[2,4,64,768]{3,2,1,0:T(8,128)(2,1)S(1)} %slice.13.own_ref), channel_id=1, source_target_pairs={{0,252},{4,0},{8,4},{12,8},{16,12},{20,16},{24,20},{28,24},{32,28}... | collective-permute-start | bytes 2359304 | tf_op jit(solution)/shard_map/ppermute | solution.py:266
  9.4 1.3 %fusion = (bf16[2,4,64,512]{3,2,1,0:T(8,128)(2,1)S(1)}, bf16[2,4,64,512]{3,2,1,0:T(8,128)(2,1)S(1)}) fusion(bf16[2,4,64,2048]{3,2,1,0:T(8,128)(2,1)} %param.6), kind=kLoop, calls=%fused_computation.1 | loop fusion | bytes 2097152 | tf_op jit(solution)/shard_map/slice | solution.py:283
  10.7 0.1 collective-permute-start.4
  10.8 5.1 %collective-permute-start.2 = (bf16[2,4,64,512]{3,2,1,0:T(8,128)(2,1)S(1)}, bf16[2,4,64,512]{3,2,1,0:T(8,128)(2,1)S(1)}, u32[]{:S(2)}, u32[]{:S(2)}) collective-permute-start(bf16[2,4,64,512]{3,2,1,0:T(8,128)(2,1)S(1)} %get-tuple-element.7.own_ref), channel_id=1, source_target_pairs={{0,252},{4,0},{8,4},{12,8},{16,12},{20,16},{24,20},{28,24},{32,28}... | collective-permute-start | bytes 1572872 | tf_op jit(solution)/shard_map/ppermute | solution.py:266
  15.9 1.0 %slice.12.own_ref = bf16[2,4,64,256]{3,2,1,0:T(8,128)(2,1)S(1)} slice(bf16[2,4,64,2048]{3,2,1,0:T(8,128)(2,1)} %param.6), slice={[0:2], [0:4], [0:64], [1280:1536]} | slice | bytes 524288 | tf_op jit(solution)/shard_map/slice | solution.py:287
  16.8 0.1 collective-permute-start
  16.9 0.1 copy.8
  17.0 0.5 %collective-permute-start.3 = (s32[6,2]{1,0:T(8,128)S(1)}, s32[6,2]{1,0:T(8,128)S(1)}, u32[]{:S(2)}, u32[]{:S(2)}) collective-permute-start(s32[6,2]{1,0:T(8,128)S(1)} %broadcast_subtract_fusion.pairs_ref), channel_id=1, source_target_pairs={{0,4},{4,8},{8,12},{12,16},{16,20},{20,24},{24,28},{28,32},{32,36}... | collective-permute-start | bytes 152 | tf_op jit(solution)/shard_map/ppermute | solution.py:266
  17.5 5.9 %collective-permute-done.3.pairs_ref = s32[6,2]{1,0:T(8,128)S(1)} collective-permute-done((s32[6,2]{1,0:T(8,128)S(1)}, s32[6,2]{1,0:T(8,128)S(1)}, u32[]{:S(2)}, u32[]{:S(2)}) %collective-permute-start.3) | collective-permute-done | bytes 80 | tf_op jit(solution)/shard_map/ppermute | solution.py:266
  23.4 2.0 %looks_last.1 = f32[2,6,16,128]{3,2,1,0:T(8,128)S(1)} custom-call(s32[6,2]{1,0:T(8,128)S(1)} %collective-permute-done.3.pairs_ref, bf16[2,4,64,512]{3,2,1,0:T(8,128)(2,1)} %collective-permute-done.4.own_ref, bf16[2,4,64,512]{3,2,1,0:T(8,128)(2,1)S(1)} %get-tuple-element.6.next_ref), custom_call_target="tpu_custom_call" | custom-call | tf_op jit(solution)/shard_map/looks_last/pallas_call | solution.py:134
  25.4 0.0 copy-start
  25.4 0.0 copy-start.1
  25.4 0.0 copy-start.2
  25.5 0.0 copy-start.3
  25.5 0.1 collective-permute-start.5
  25.6 1.6 %looks_part.3.refs_1_ = f32[2,6,16,128]{3,2,1,0:T(8,128)S(1)} custom-call(s32[6,2]{1,0:T(8,128)S(1)} %broadcast_subtract_fusion.pairs_ref, bf16[2,4,64,512]{3,2,1,0:T(8,128)(2,1)S(1)} %get-tuple-element.7.own_ref, bf16[2,4,64,512]{3,2,1,0:T(8,128)(2,1)S(1)} %collective-permute-done.2.next_ref), custom_call_target="tpu_custom_call" | custom-call | tf_op jit(solution)/shard_map/looks_part/pallas_call | solution.py:134
  27.1 2.1 %looks_part.2.refs_0_ = f32[2,6,16,128]{3,2,1,0:T(8,128)S(1)} custom-call(s32[6,2]{1,0:T(8,128)S(1)} %broadcast_subtract_fusion.pairs_ref, bf16[2,4,64,768]{3,2,1,0:T(8,128)(2,1)S(1)} %slice.13.own_ref, bf16[2,4,64,768]{3,2,1,0:T(8,128)(2,1)S(1)} %collective-permute-done.1.next_ref), custom_call_target="tpu_custom_call" | custom-call | tf_op jit(solution)/shard_map/looks_part/pallas_call | solution.py:134
  29.3 2.1 %looks_end.1 = (f32[2,6,16,128]{3,2,1,0:T(8,128)S(1)}, f32[6,16,128]{2,1,0:T(8,128)}) custom-call(s32[6,2]{1,0:T(8,128)S(1)} %broadcast_subtract_fusion.pairs_ref, bf16[2,4,64,256]{3,2,1,0:T(8,128)(2,1)S(1)} %slice.12.own_ref, bf16[2,4,64,256]{3,2,1,0:T(8,128)(2,1)} %collective-permute-done.next_ref, f32[2,6,16,128]{3,2,1,0:T(8,128)S(1)} %looks_part.2.refs_0_, ...), custom_call_target="tpu_custom_call" | custom-call | tf_op jit(solution)/shard_map/looks_end/pallas_call | solution.py:134
  31.4 1.3 %collective-permute-start.6 = (f32[2,6,16,128]{3,2,1,0:T(8,128)S(1)}, f32[2,6,16,128]{3,2,1,0:T(8,128)S(1)}, u32[]{:S(2)}, u32[]{:S(2)}) collective-permute-start(f32[2,6,16,128]{3,2,1,0:T(8,128)S(1)} %get-tuple-element.5.own_ref), channel_id=1, source_target_pairs={{0,1},{2,3},{1,0},{3,2},{4,5},{6,7},{5,4},{7,6},{8,9},{10,11},{9,8... | collective-permute-start | bytes 294920 | tf_op jit(solution)/shard_map/ppermute | solution.py:272
  32.7 1.9 %collective-permute-start.7 = (f32[2,6,16,128]{3,2,1,0:T(8,128)S(1)}, f32[2,6,16,128]{3,2,1,0:T(8,128)S(1)}, u32[]{:S(2)}, u32[]{:S(2)}) collective-permute-start(f32[2,6,16,128]{3,2,1,0:T(8,128)S(1)} %get-tuple-element.5.own_ref), channel_id=1, source_target_pairs={{1,2},{2,1},{5,6},{6,5},{9,10},{10,9},{13,14},{14,13},{17,18},{18,... | collective-permute-start | bytes 294920 | tf_op jit(solution)/shard_map/ppermute | solution.py:272
  34.6 2.0 %collective-permute-done.6.near_ref = f32[2,6,16,128]{3,2,1,0:T(8,128)S(1)} collective-permute-done((f32[2,6,16,128]{3,2,1,0:T(8,128)S(1)}, f32[2,6,16,128]{3,2,1,0:T(8,128)S(1)}, u32[]{:S(2)}, u32[]{:S(2)}) %collective-permute-start.6) | collective-permute-done | bytes 98336 | tf_op jit(solution)/shard_map/ppermute | solution.py:272
  36.6 2.9 %collective-permute-done.7.far_ref = f32[2,6,16,128]{3,2,1,0:T(8,128)S(1)} collective-permute-done((f32[2,6,16,128]{3,2,1,0:T(8,128)S(1)}, f32[2,6,16,128]{3,2,1,0:T(8,128)S(1)}, u32[]{:S(2)}, u32[]{:S(2)}) %collective-permute-start.7) | collective-permute-done | bytes 98336 | tf_op jit(solution)/shard_map/ppermute | solution.py:272
  39.5 3.4 %goldstein.1 = f32[2,6,16,128]{3,2,1,0:T(8,128)} custom-call(s32[1]{0:T(128)} %bitcast.odd_ref, f32[2,6,16,128]{3,2,1,0:T(8,128)S(1)} %collective-permute-done.6.near_ref, f32[2,6,16,128]{3,2,1,0:T(8,128)S(1)} %get-tuple-element.5.own_ref, f32[2,6,16,128]{3,2,1,0:T(8,128)S(1)} %collective-permute-done.7.far_ref, bf16[128,288]{1,0:T(8,128)(2,1)S(1)} %copy-done.1, ...), custom_call_target="tpu_custom_call" | custom-call | tf_op jit(solution)/shard_map/goldstein/pallas_call | solution.py:246
  (12 shorter events, 0.0 us)
Async XLA Ops:
  0.6 16.3 %copy-start.4 = (s32[6,2]{0,1:T(2,128)S(1)}, s32[6,2]{0,1:T(2,128)}, u32[]{:S(2)}) copy-start(s32[6,2]{0,1:T(2,128)} %param.7) | copy-start | bytes 148
  1.8 25.3 %collective-permute-start.1 = (bf16[2,4,64,768]{3,2,1,0:T(8,128)(2,1)S(1)}, bf16[2,4,64,768]{3,2,1,0:T(8,128)(2,1)S(1)}, u32[]{:S(2)}, u32[]{:S(2)}) collective-permute-start(bf16[2,4,64,768]{3,2,1,0:T(8,128)(2,1)S(1)} %slice.13.own_ref), channel_id=1, source_target_pairs={{0,252},{4,0},{8,4},{12,8},{16,12},{20,16},{24,20},{28,24},{32,28}... | collective-permute-start | bytes 2359304 | tf_op jit(solution)/shard_map/ppermute | solution.py:266
  10.7 12.7 %collective-permute-start.4 = (bf16[2,4,64,512]{3,2,1,0:T(8,128)(2,1)S(1)}, bf16[2,4,64,512]{3,2,1,0:T(8,128)(2,1)}, u32[]{:S(2)}, u32[]{:S(2)}) collective-permute-start(bf16[2,4,64,512]{3,2,1,0:T(8,128)(2,1)S(1)} %get-tuple-element.6.next_ref), channel_id=1, source_target_pairs={{0,4},{4,8},{8,12},{12,16},{16,20},{20,24},{24,28},{28,32},{32,36}... | collective-permute-start | bytes 1572872 | tf_op jit(solution)/shard_map/ppermute | solution.py:266
  10.8 14.8 %collective-permute-start.2 = (bf16[2,4,64,512]{3,2,1,0:T(8,128)(2,1)S(1)}, bf16[2,4,64,512]{3,2,1,0:T(8,128)(2,1)S(1)}, u32[]{:S(2)}, u32[]{:S(2)}) collective-permute-start(bf16[2,4,64,512]{3,2,1,0:T(8,128)(2,1)S(1)} %get-tuple-element.7.own_ref), channel_id=1, source_target_pairs={{0,252},{4,0},{8,4},{12,8},{16,12},{20,16},{24,20},{28,24},{32,28}... | collective-permute-start | bytes 1572872 | tf_op jit(solution)/shard_map/ppermute | solution.py:266
  16.8 12.4 %collective-permute-start = (bf16[2,4,64,256]{3,2,1,0:T(8,128)(2,1)S(1)}, bf16[2,4,64,256]{3,2,1,0:T(8,128)(2,1)}, u32[]{:S(2)}, u32[]{:S(2)}) collective-permute-start(bf16[2,4,64,256]{3,2,1,0:T(8,128)(2,1)S(1)} %slice.12.own_ref), channel_id=1, source_target_pairs={{0,252},{4,0},{8,4},{12,8},{16,12},{20,16},{24,20},{28,24},{32,28}... | collective-permute-start | bytes 786440 | tf_op jit(solution)/shard_map/ppermute | solution.py:266
  17.0 6.4 %collective-permute-start.3 = (s32[6,2]{1,0:T(8,128)S(1)}, s32[6,2]{1,0:T(8,128)S(1)}, u32[]{:S(2)}, u32[]{:S(2)}) collective-permute-start(s32[6,2]{1,0:T(8,128)S(1)} %broadcast_subtract_fusion.pairs_ref), channel_id=1, source_target_pairs={{0,4},{4,8},{8,12},{12,16},{16,20},{20,24},{24,28},{28,32},{32,36}... | collective-permute-start | bytes 152 | tf_op jit(solution)/shard_map/ppermute | solution.py:266
  25.4 14.0 %copy-start = (bf16[4,128,128]{2,1,0:T(8,128)(2,1)S(1)}, bf16[4,128,128]{2,1,0:T(8,128)(2,1)}, u32[]{:S(2)}) copy-start(bf16[4,128,128]{2,1,0:T(8,128)(2,1)} %constant.35.clone.back_ref) | copy-start | bytes 393220
  25.4 14.0 %copy-start.1 = (bf16[128,288]{1,0:T(8,128)(2,1)S(1)}, bf16[128,288]{1,0:T(8,128)(2,1)}, u32[]{:S(2)}) copy-start(bf16[128,288]{1,0:T(8,128)(2,1)} %constant.32.clone.rows_ref) | copy-start | bytes 221188
  25.4 14.0 %copy-start.2 = (bf16[4,32,128]{2,1,0:T(8,128)(2,1)S(1)}, bf16[4,32,128]{2,1,0:T(8,128)(2,1)}, u32[]{:S(2)}) copy-start(bf16[4,32,128]{2,1,0:T(8,128)(2,1)} %constant.34.clone.fore_ref) | copy-start | bytes 98308
  25.5 14.0 %copy-start.3 = (bf16[32,384]{1,0:T(8,128)(2,1)S(1)}, bf16[32,384]{1,0:T(8,128)(2,1)}, u32[]{:S(2)}) copy-start(bf16[32,384]{1,0:T(8,128)(2,1)} %constant.33.clone.final_ref) | copy-start | bytes 73732
  25.5 3.8 %collective-permute-start.5 = (f32[2,6,16,128]{3,2,1,0:T(8,128)S(1)}, f32[2,6,16,128]{3,2,1,0:T(8,128)S(1)}, u32[]{:S(2)}, u32[]{:S(2)}) collective-permute-start(f32[2,6,16,128]{3,2,1,0:T(8,128)S(1)} %looks_last.1), channel_id=1, source_target_pairs={{0,252},{4,0},{8,4},{12,8},{16,12},{20,16},{24,20},{28,24},{32,28}... | collective-permute-start | bytes 294920 | tf_op jit(solution)/shard_map/ppermute | solution.py:266
  31.4 5.2 %collective-permute-start.6 = (f32[2,6,16,128]{3,2,1,0:T(8,128)S(1)}, f32[2,6,16,128]{3,2,1,0:T(8,128)S(1)}, u32[]{:S(2)}, u32[]{:S(2)}) collective-permute-start(f32[2,6,16,128]{3,2,1,0:T(8,128)S(1)} %get-tuple-element.5.own_ref), channel_id=1, source_target_pairs={{0,1},{2,3},{1,0},{3,2},{4,5},{6,7},{5,4},{7,6},{8,9},{10,11},{9,8... | collective-permute-start | bytes 294920 | tf_op jit(solution)/shard_map/ppermute | solution.py:272
  32.7 6.8 %collective-permute-start.7 = (f32[2,6,16,128]{3,2,1,0:T(8,128)S(1)}, f32[2,6,16,128]{3,2,1,0:T(8,128)S(1)}, u32[]{:S(2)}, u32[]{:S(2)}) collective-permute-start(f32[2,6,16,128]{3,2,1,0:T(8,128)S(1)} %get-tuple-element.5.own_ref), channel_id=1, source_target_pairs={{1,2},{2,1},{5,6},{6,5},{9,10},{10,9},{13,14},{14,13},{17,18},{18,... | collective-permute-start | bytes 294920 | tf_op jit(solution)/shard_map/ppermute | solution.py:272

commit v2 on v1

--- a/solution.py
+++ b/solution.py
@@ -56,16 +56,10 @@
     )
 
 
-def looks_kernel(pairs_ref, own_ref, next_ref, *refs, start, added, coherence):
-    extra, refs = refs[:added], refs[added:]
-    gamma_ref, refs = refs[0], refs[1:]
-    if coherence:
-        coherence_ref, refs = refs[0], refs[1:]
-    images, terms, total, power = refs
-    chunks = own_ref.shape[-1] // 256
+def pool_terms(pairs_ref, own_ref, next_ref, start, images, terms, total):
     count = pairs_ref.shape[0]
     half = terms.shape[1] // 2
-    for c in range(chunks):
+    for c in range(own_ref.shape[-1] // 256):
         slot = c % 2
         for date in range(4):
             for part in range(2):
@@ -105,8 +99,40 @@
         sample = lax.broadcasted_iota(jnp.int32, (256, 128), 0)
         column = lax.broadcasted_iota(jnp.int32, (256, 128), 1)
         pool = ((sample >> 4) + (start // 16 + 16 * c) == column).astype(F32).astype(BF16)
-        part = jnp.dot(terms[slot], pool, preferred_element_type=F32)
-        total[...] = part if c == 0 else total[...] + part
+        total[...] += jnp.dot(terms[slot], pool, preferred_element_type=F32)
+
+
+def fetch(sources, targets, sems):
+    return [
+        pltpu.make_async_copy(source, target, sems.at[i])
+        for i, (source, target) in enumerate(zip(sources, targets))
+    ]
+
+
+def looks_kernel(*refs, start, tables, added, final):
+    take = iter(refs)
+    pairs_ref, own_ref, next_ref = (next(take) for _ in range(3))
+    flag_ref, last_ref = (next(take), next(take)) if final else (None, None)
+    extra = [next(take) for _ in range(added)]
+    sources = [next(take) for _ in range(tables)]
+    gamma_ref = next(take)
+    coherence_ref = next(take) if final else None
+    targets = [next(take) for _ in range(tables)]
+    images, terms, total, power = (next(take) for _ in range(4))
+    copies = fetch(sources, targets, next(take)) if tables else []
+    for copy in copies:
+        copy.start()
+    count = pairs_ref.shape[0]
+    half = terms.shape[1] // 2
+    total[...] = jnp.zeros_like(total)
+    pool_terms(pairs_ref, own_ref, next_ref, start, images, terms, total)
+    if final:
+
+        @pl.when(flag_ref[0] == 1)
+        def _():
+            edge = 2048 - last_ref.shape[-1]
+            pool_terms(pairs_ref, last_ref, last_ref, edge, images, terms, total)
+
     power[...] = (
         total[pl.ds(32 * count, 128)] + total[pl.ds(half + 32 * count, 128)]
     ).reshape(8, 16, 128) * (1.0 / 64.0)
@@ -120,31 +146,44 @@
             re, im = re + ref[0, p], im + ref[1, p]
         gamma_ref[0, p] = re
         gamma_ref[1, p] = im
-        if coherence:
+        if final:
             coherence_ref[p] = jnp.sqrt(re * re + im * im)
-
-
-def looks(pairs, own, following, start, extra=(), coherence=False, name="looks"):
+    for copy in copies:
+        copy.wait()
+
+
+def looks(pairs, own, following, start, name, last=None, extra=(), tables=()):
     count = pairs.shape[0]
     rows = 16 * (2 * count + 8)
     vmem = pl.BlockSpec(memory_space=pltpu.VMEM)
+    smem = pl.BlockSpec(memory_space=pltpu.SMEM)
+    final = last is not None
     shapes = [jax.ShapeDtypeStruct((2, count, 16, 128), F32)]
-    if coherence:
+    if final:
         shapes.append(jax.ShapeDtypeStruct((count, 16, 128), F32))
+    shapes += [jax.ShapeDtypeStruct(table.shape, table.dtype) for table in tables]
+    scratch = [
+        pltpu.VMEM((2, 8, 2, 2, 64, 128), F32),
+        pltpu.VMEM((2, 2 * rows, 256), BF16),
+        pltpu.VMEM((2 * rows, 128), F32),
+        pltpu.VMEM((8, 16, 128), F32),
+    ]
+    if tables:
+        scratch.append(pltpu.SemaphoreType.DMA((len(tables),)))
     return pl.pallas_call(
-        functools.partial(looks_kernel, start=start, added=len(extra), coherence=coherence),
+        functools.partial(
+            looks_kernel, start=start, tables=len(tables), added=len(extra), final=final
+        ),
         out_shape=shapes,
-        in_specs=[pl.BlockSpec(memory_space=pltpu.SMEM)] + [vmem] * (2 + len(extra)),
+        in_specs=[smem, vmem, vmem]
+        + ([smem, vmem] if final else [])
+        + [vmem] * len(extra)
+        + [pl.BlockSpec(memory_space=pl.ANY)] * len(tables),
         out_specs=[vmem] * len(shapes),
-        scratch_shapes=[
-            pltpu.VMEM((2, 8, 2, 2, 64, 128), F32),
-            pltpu.VMEM((2, 2 * rows, 256), BF16),
-            pltpu.VMEM((2 * rows, 128), F32),
-            pltpu.VMEM((8, 16, 128), F32),
-        ],
+        scratch_shapes=scratch,
         compiler_params=pltpu.CompilerParams(vmem_limit_bytes=12 << 20),
         name=name,
-    )(pairs, own, following, *extra)
+    )(pairs, own, following, *(last or ()), *extra, *tables)
 
 
 def ring(power, axis, step, index):
@@ -263,6 +302,11 @@
 
 def shifted(value, axis, step):
     size = lax.axis_size(axis)
+    return lax.ppermute(value, axis, [(i, i + step) for i in range(size) if 0 <= i + step < size])
+
+
+def turned(value, axis, step):
+    size = lax.axis_size(axis)
     return lax.ppermute(value, axis, [(i, (i + step) % size) for i in range(size)])
 
 
@@ -272,7 +316,11 @@
     return lax.ppermute(value, axis, pairs + [(j, i) for i, j in pairs])
 
 
-COLUMNS = (768, 512, 256)
+COLUMNS = (1024, 512)
+
+
+def after(value, *done):
+    return lax.optimization_barrier((value, *done))[0]
 
 
 def per_device(slc, pairs):
@@ -280,22 +328,26 @@
     block = lax.axis_index("date")
     here = pairs - block * dates
     edge = sum(COLUMNS)
+    ends = np.cumsum((0, *COLUMNS))
+    own = [slc[..., at : at + width] for at, width in zip(ends, COLUMNS)]
     own_last = slc[..., edge:]
+    following = [turned(piece, "date", -1) for piece in own]
     previous_last = shifted(own_last, "date", 1)
-    own, following, starts, at = [], [], [], 0
-    for width in COLUMNS:
-        own.append(slc[..., at : at + width])
-        following.append(shifted(own[-1], "date", -1))
-        starts.append(at)
-        at += width
     there = shifted(here, "date", 1)
-    [returned] = looks(there, previous_last, own_last, edge, name="looks_last")
-    returned = shifted(returned, "date", -1)
+    there = jnp.clip(there, 0, 2 * dates - 1)
     parts = []
-    for k in range(len(COLUMNS) - 1):
-        parts += looks(here, own[k], following[k], starts[k], name="looks_part")
+    if False:
+        parts += looks(here, own[0], following[0], 0, "looks_part")
+        there = after(there, parts[0])
+    [last_part] = looks(there, previous_last, own_last, edge, "looks_last")
+    returned = shifted(last_part, "date", -1)
+    here = after(here, last_part)
+    for k in range(len(parts), len(COLUMNS) - 1):
+        parts += looks(here, own[k], following[k], int(ends[k]), "looks_part")
+    is_last = (block == lax.axis_size("date") - 1).astype(jnp.int32).reshape(1)
     gamma, coherence = looks(
-        here, own[-1], following[-1], starts[-1], (*parts, returned), True, name="looks_end"
+        here, own[-1], following[-1], int(ends[-2]), "looks_end",
+        last=(is_last, own_last), extra=(*parts, returned),
     )
     near = swapped(gamma, "space", 0)
     far = swapped(gamma, "space", 1)

time: 43.1 us -> 42 us (0.974)
  local copies, waits for them, and re-layouts: 3.58 us -> 1.71 us
  waiting for transfers between devices: 10.8 us -> 11.7 us
  Pallas kernels: 11.2 us -> 10.7 us
    slice x3 -> x2, local copies, waits for them, and re-layouts: 3.45 us -> 1.59 us  [per_device(): own = [slc[..., at:at + width] for at, width in zip(ends, COLUMNS)]]
    ppermute x6 -> x5, waiting for transfers between devices: 5.89 us -> 7.09 us  [the longest x2 6.28 us: turned(): lax.ppermute(value, axis, [(i, (i + step) % size) for i in range(size)])]
    pallas_call x4 -> x3, Pallas kernels: 7.78 us -> 7.3 us  [looks(): pl.pallas_call(functools.partial(looks_kernel, start=start, tables=len(ta...]
    ppermute x6 -> x5, starting transfers between devices: 13.4 us -> 13.5 us  [the longest x2 7.57 us: turned(): lax.ppermute(value, axis, [(i, (i + step) % size) for i in range(size)])]
  transfers between devices with their start and end apart: 8 -> 7, of which waited for: 3 -> 5; matrix products, arithmetic and copies ran while one was open for 5% -> 1% of each run, Pallas kernels for 13% -> 11%
where the time goes in v2:
time: 42 us; the launch traced here: 41.5 us
  starting transfers between devices  16.7 us (40%)
  waiting for transfers between devices  11.7 us (28%)
  Pallas kernels  10.7 us (25%)
  local copies, waits for them, and re-layouts  1.71 us (4%)
  between operations  0.77 us (2%)
    ppermute x2, starting transfers between devices, turned(): lax.ppermute(value, axis, [(i, (i + step) % size) for i in range(size)])  7.57 us
    pallas_call x3, Pallas kernels, looks(): pl.pallas_call(functools.partial(looks_kernel, start=start, tables=len(ta...  7.3 us
    ppermute x2, waiting for transfers between devices, turned(): lax.ppermute(value, axis, [(i, (i + step) % size) for i in range(size)])  6.28 us
    ppermute x3, starting transfers between devices, shifted(): lax.ppermute(value, axis, [(i, i + step) for i in range(size) if 0 <= i +...  5.93 us
    ppermute x2, waiting for transfers between devices, swapped(): return lax.ppermute(value, axis, pairs + [(j, i) for i, j in pairs])  4.57 us
    pallas_call x1, Pallas kernels, goldstein(): pl.pallas_call(filter_kernel, out_shape=jax.ShapeDtypeStruct((2, count, 1...  3.38 us
    ppermute x2, starting transfers between devices, swapped(): return lax.ppermute(value, axis, pairs + [(j, i) for i, j in pairs])  3.19 us
    slice x2, local copies, waits for them, and re-layouts, per_device(): own = [slc[..., at:at + width] for at, width in zip(ends, COLUMNS)]  1.59 us
  transfers between devices with their start and end apart: 7, of which 5 were waited for; matrix products, arithmetic and copies ran while one was open for 1% of the time, Pallas kernels for 11%

profile of v2, /device:TPU:16, one launch (start us, length us, event | category | flops | bytes accessed | tf_op | source)
XLA Modules:
  0.0 41.5 jit_solution(4294893713939704714)
XLA Ops:
  0.6 1.5 %slice.11.refs_1_ = bf16[2,4,64,1024]{3,2,1,0:T(8,128)(2,1)S(1)} slice(bf16[2,4,64,2048]{3,2,1,0:T(8,128)(2,1)} %param.6), slice={[0:2], [0:4], [0:64], [0:1024]} | slice | bytes 2097152 | tf_op jit(solution)/shard_map/slice | solution.py:332
  2.1 7.6 %collective-permute-start.3 = (bf16[2,4,64,1024]{3,2,1,0:T(8,128)(2,1)S(1)}, bf16[2,4,64,1024]{3,2,1,0:T(8,128)(2,1)S(1)}, u32[]{:S(2)}, u32[]{:S(2)}) collective-permute-start(bf16[2,4,64,1024]{3,2,1,0:T(8,128)(2,1)S(1)} %slice.11.refs_1_), channel_id=1, source_target_pairs={{0,252},{4,0},{8,4},{12,8},{16,12},{20,16},{24,20},{28,24},{32,28}... | collective-permute-start | bytes 3145736 | tf_op jit(solution)/shard_map/ppermute | solution.py:310
  9.7 0.1 fusion
  9.8 2.1 %collective-permute-start.1 = (bf16[2,4,64,512]{3,2,1,0:T(8,128)(2,1)S(1)}, bf16[2,4,64,512]{3,2,1,0:T(8,128)(2,1)}, u32[]{:S(2)}, u32[]{:S(2)}) collective-permute-start(bf16[2,4,64,512]{3,2,1,0:T(8,128)(2,1)S(1)} %get-tuple-element.9.refs_2_.refs_4_), channel_id=1, source_target_pairs={{0,4},{4,8},{8,12},{12,16},{16,20},{20,24},{24,28},{28,32},{32,36}... | collective-permute-start | bytes 1572872 | tf_op jit(solution)/shard_map/ppermute | solution.py:305
  11.9 0.0 collective-permute-start.2
  11.9 0.1 copy.8
  12.0 2.4 %collective-permute-start = (s32[6,2]{1,0:T(8,128)S(1)}, s32[6,2]{1,0:T(8,128)S(1)}, u32[]{:S(2)}, u32[]{:S(2)}) collective-permute-start(s32[6,2]{1,0:T(8,128)S(1)} %broadcast_subtract_fusion.refs_0_), channel_id=1, source_target_pairs={{0,4},{4,8},{8,12},{12,16},{16,20},{20,24},{24,28},{28,32},{32,36}... | collective-permute-start | bytes 152 | tf_op jit(solution)/shard_map/ppermute | solution.py:305
  14.4 0.8 %collective-permute-done = s32[6,2]{1,0:T(8,128)S(1)} collective-permute-done((s32[6,2]{1,0:T(8,128)S(1)}, s32[6,2]{1,0:T(8,128)S(1)}, u32[]{:S(2)}, u32[]{:S(2)}) %collective-permute-start) | collective-permute-done | bytes 80 | tf_op jit(solution)/shard_map/ppermute | solution.py:305
  15.2 2.0 %looks_last.1 = f32[2,6,16,128]{3,2,1,0:T(8,128)S(1)} custom-call(s32[6,2]{1,0:T(8,128)S(1)} %broadcast_clamp_fusion.refs_0_, bf16[2,4,64,512]{3,2,1,0:T(8,128)(2,1)} %collective-permute-done.1.refs_1_, bf16[2,4,64,512]{3,2,1,0:T(8,128)(2,1)S(1)} %get-tuple-element.9.refs_2_.refs_4_), custom_call_target="tpu_custom_call" | custom-call | tf_op jit(solution)/shard_map/looks_last/pallas_call | solution.py:173
  17.3 0.0 copy-start
  17.3 0.0 copy-start.1
  17.3 0.0 copy-start.2
  17.3 0.0 copy-start.3
  17.3 1.4 %collective-permute-start.4 = (f32[2,6,16,128]{3,2,1,0:T(8,128)S(1)}, f32[2,6,16,128]{3,2,1,0:T(8,128)}, u32[]{:S(2)}, u32[]{:S(2)}) collective-permute-start(f32[2,6,16,128]{3,2,1,0:T(8,128)S(1)} %looks_last.1), channel_id=1, source_target_pairs={{4,0},{8,4},{12,8},{16,12},{20,16},{24,20},{28,24},{32,28},{36,32}... | collective-permute-start | bytes 294920 | tf_op jit(solution)/shard_map/ppermute | solution.py:305
  18.8 3.3 %collective-permute-done.3.refs_2_ = bf16[2,4,64,1024]{3,2,1,0:T(8,128)(2,1)S(1)} collective-permute-done((bf16[2,4,64,1024]{3,2,1,0:T(8,128)(2,1)S(1)}, bf16[2,4,64,1024]{3,2,1,0:T(8,128)(2,1)S(1)}, u32[]{:S(2)}, u32[]{:S(2)}) %collective-permute-start.3) | collective-permute-done | bytes 1048608 | tf_op jit(solution)/shard_map/ppermute | solution.py:310
  22.0 2.6 %looks_part.1.refs_5_ = f32[2,6,16,128]{3,2,1,0:T(8,128)S(1)} custom-call(s32[6,2]{1,0:T(8,128)S(1)} %broadcast_subtract_fusion.refs_0_, bf16[2,4,64,1024]{3,2,1,0:T(8,128)(2,1)S(1)} %slice.11.refs_1_, bf16[2,4,64,1024]{3,2,1,0:T(8,128)(2,1)S(1)} %collective-permute-done.3.refs_2_), custom_call_target="tpu_custom_call" | custom-call | tf_op jit(solution)/shard_map/looks_part/pallas_call | solution.py:173
  24.6 3.0 %collective-permute-done.2.refs_2_ = bf16[2,4,64,512]{3,2,1,0:T(8,128)(2,1)} collective-permute-done((bf16[2,4,64,512]{3,2,1,0:T(8,128)(2,1)S(1)}, bf16[2,4,64,512]{3,2,1,0:T(8,128)(2,1)}, u32[]{:S(2)}, u32[]{:S(2)}) %collective-permute-start.2) | collective-permute-done | bytes 524320 | tf_op jit(solution)/shard_map/ppermute | solution.py:310
  27.6 0.0 collective-permute-done.4.refs_6_
  27.6 2.7 %looks_end.1 = (f32[2,6,16,128]{3,2,1,0:T(8,128)S(1)}, f32[6,16,128]{2,1,0:T(8,128)}) custom-call(s32[6,2]{1,0:T(8,128)S(1)} %broadcast_subtract_fusion.refs_0_, bf16[2,4,64,512]{3,2,1,0:T(8,128)(2,1)S(1)} %get-tuple-element.8.refs_1_, bf16[2,4,64,512]{3,2,1,0:T(8,128)(2,1)} %collective-permute-done.2.refs_2_, s32[1]{0:T(128)} %bitcast.refs_3_, ...), custom_call_target="tpu_custom_call" | custom-call | tf_op jit(solution)/shard_map/looks_end/pallas_call | solution.py:173
  30.3 1.3 %collective-permute-start.5 = (f32[2,6,16,128]{3,2,1,0:T(8,128)S(1)}, f32[2,6,16,128]{3,2,1,0:T(8,128)S(1)}, u32[]{:S(2)}, u32[]{:S(2)}) collective-permute-start(f32[2,6,16,128]{3,2,1,0:T(8,128)S(1)} %get-tuple-element.7.own_ref), channel_id=1, source_target_pairs={{0,1},{2,3},{1,0},{3,2},{4,5},{6,7},{5,4},{7,6},{8,9},{10,11},{9,8... | collective-permute-start | bytes 294920 | tf_op jit(solution)/shard_map/ppermute | solution.py:316
  31.6 1.9 %collective-permute-start.6 = (f32[2,6,16,128]{3,2,1,0:T(8,128)S(1)}, f32[2,6,16,128]{3,2,1,0:T(8,128)S(1)}, u32[]{:S(2)}, u32[]{:S(2)}) collective-permute-start(f32[2,6,16,128]{3,2,1,0:T(8,128)S(1)} %get-tuple-element.7.own_ref), channel_id=1, source_target_pairs={{1,2},{2,1},{5,6},{6,5},{9,10},{10,9},{13,14},{14,13},{17,18},{18,... | collective-permute-start | bytes 294920 | tf_op jit(solution)/shard_map/ppermute | solution.py:316
  33.6 1.4 %collective-permute-done.5.near_ref = f32[2,6,16,128]{3,2,1,0:T(8,128)S(1)} collective-permute-done((f32[2,6,16,128]{3,2,1,0:T(8,128)S(1)}, f32[2,6,16,128]{3,2,1,0:T(8,128)S(1)}, u32[]{:S(2)}, u32[]{:S(2)}) %collective-permute-start.5) | collective-permute-done | bytes 98336 | tf_op jit(solution)/shard_map/ppermute | solution.py:316
  35.0 3.2 %collective-permute-done.6.far_ref = f32[2,6,16,128]{3,2,1,0:T(8,128)S(1)} collective-permute-done((f32[2,6,16,128]{3,2,1,0:T(8,128)S(1)}, f32[2,6,16,128]{3,2,1,0:T(8,128)S(1)}, u32[]{:S(2)}, u32[]{:S(2)}) %collective-permute-start.6) | collective-permute-done | bytes 98336 | tf_op jit(solution)/shard_map/ppermute | solution.py:316
  38.1 3.4 %goldstein.1 = f32[2,6,16,128]{3,2,1,0:T(8,128)} custom-call(s32[1]{0:T(128)} %bitcast.1.odd_ref, f32[2,6,16,128]{3,2,1,0:T(8,128)S(1)} %collective-permute-done.5.near_ref, f32[2,6,16,128]{3,2,1,0:T(8,128)S(1)} %get-tuple-element.7.own_ref, f32[2,6,16,128]{3,2,1,0:T(8,128)S(1)} %collective-permute-done.6.far_ref, bf16[128,288]{1,0:T(8,128)(2,1)S(1)} %copy-done.1, ...), custom_call_target="tpu_custom_call" | custom-call | tf_op jit(solution)/shard_map/goldstein/pallas_call | solution.py:285
  (11 shorter events, 0.0 us)
Async XLA Ops:
  0.6 9.1 %copy-start.4 = (bf16[2,4,64,2048]{3,2,1,0:T(8,128)(2,1)S(1)}, bf16[2,4,64,2048]{3,2,1,0:T(8,128)(2,1)}, u32[]{:S(2)}) copy-start(bf16[2,4,64,2048]{3,2,1,0:T(8,128)(2,1)} %param.6) | copy-start | bytes 6291460
  0.6 11.3 %copy-start.5 = (s32[6,2]{0,1:T(2,128)S(1)}, s32[6,2]{0,1:T(2,128)}, u32[]{:S(2)}) copy-start(s32[6,2]{0,1:T(2,128)} %param.7) | copy-start | bytes 148
  2.1 19.9 %collective-permute-start.3 = (bf16[2,4,64,1024]{3,2,1,0:T(8,128)(2,1)S(1)}, bf16[2,4,64,1024]{3,2,1,0:T(8,128)(2,1)S(1)}, u32[]{:S(2)}, u32[]{:S(2)}) collective-permute-start(bf16[2,4,64,1024]{3,2,1,0:T(8,128)(2,1)S(1)} %slice.11.refs_1_), channel_id=1, source_target_pairs={{0,252},{4,0},{8,4},{12,8},{16,12},{20,16},{24,20},{28,24},{32,28}... | collective-permute-start | bytes 3145736 | tf_op jit(solution)/shard_map/ppermute | solution.py:310
  9.8 5.4 %collective-permute-start.1 = (bf16[2,4,64,512]{3,2,1,0:T(8,128)(2,1)S(1)}, bf16[2,4,64,512]{3,2,1,0:T(8,128)(2,1)}, u32[]{:S(2)}, u32[]{:S(2)}) collective-permute-start(bf16[2,4,64,512]{3,2,1,0:T(8,128)(2,1)S(1)} %get-tuple-element.9.refs_2_.refs_4_), channel_id=1, source_target_pairs={{0,4},{4,8},{8,12},{12,16},{16,20},{20,24},{24,28},{28,32},{32,36}... | collective-permute-start | bytes 1572872 | tf_op jit(solution)/shard_map/ppermute | solution.py:305
  11.9 15.7 %collective-permute-start.2 = (bf16[2,4,64,512]{3,2,1,0:T(8,128)(2,1)S(1)}, bf16[2,4,64,512]{3,2,1,0:T(8,128)(2,1)}, u32[]{:S(2)}, u32[]{:S(2)}) collective-permute-start(bf16[2,4,64,512]{3,2,1,0:T(8,128)(2,1)S(1)} %get-tuple-element.8.refs_1_), channel_id=1, source_target_pairs={{0,252},{4,0},{8,4},{12,8},{16,12},{20,16},{24,20},{28,24},{32,28}... | collective-permute-start | bytes 1572872 | tf_op jit(solution)/shard_map/ppermute | solution.py:310
  12.0 3.2 %collective-permute-start = (s32[6,2]{1,0:T(8,128)S(1)}, s32[6,2]{1,0:T(8,128)S(1)}, u32[]{:S(2)}, u32[]{:S(2)}) collective-permute-start(s32[6,2]{1,0:T(8,128)S(1)} %broadcast_subtract_fusion.refs_0_), channel_id=1, source_target_pairs={{0,4},{4,8},{8,12},{12,16},{16,20},{20,24},{24,28},{28,32},{32,36}... | collective-permute-start | bytes 152 | tf_op jit(solution)/shard_map/ppermute | solution.py:305
  17.3 20.9 %copy-start = (bf16[4,128,128]{2,1,0:T(8,128)(2,1)S(1)}, bf16[4,128,128]{2,1,0:T(8,128)(2,1)}, u32[]{:S(2)}) copy-start(bf16[4,128,128]{2,1,0:T(8,128)(2,1)} %constant.40.clone.back_ref) | copy-start | bytes 393220
  17.3 20.8 %copy-start.1 = (bf16[128,288]{1,0:T(8,128)(2,1)S(1)}, bf16[128,288]{1,0:T(8,128)(2,1)}, u32[]{:S(2)}) copy-start(bf16[128,288]{1,0:T(8,128)(2,1)} %constant.37.clone.rows_ref) | copy-start | bytes 221188
  17.3 20.8 %copy-start.2 = (bf16[4,32,128]{2,1,0:T(8,128)(2,1)S(1)}, bf16[4,32,128]{2,1,0:T(8,128)(2,1)}, u32[]{:S(2)}) copy-start(bf16[4,32,128]{2,1,0:T(8,128)(2,1)} %constant.39.clone.fore_ref) | copy-start | bytes 98308
  17.3 20.8 %copy-start.3 = (bf16[32,384]{1,0:T(8,128)(2,1)S(1)}, bf16[32,384]{1,0:T(8,128)(2,1)}, u32[]{:S(2)}) copy-start(bf16[32,384]{1,0:T(8,128)(2,1)} %constant.38.clone.final_ref) | copy-start | bytes 73732
  17.3 10.3 %collective-permute-start.4 = (f32[2,6,16,128]{3,2,1,0:T(8,128)S(1)}, f32[2,6,16,128]{3,2,1,0:T(8,128)}, u32[]{:S(2)}, u32[]{:S(2)}) collective-permute-start(f32[2,6,16,128]{3,2,1,0:T(8,128)S(1)} %looks_last.1), channel_id=1, source_target_pairs={{4,0},{8,4},{12,8},{16,12},{20,16},{24,20},{28,24},{32,28},{36,32}... | collective-permute-start | bytes 294920 | tf_op jit(solution)/shard_map/ppermute | solution.py:305
  30.3 4.6 %collective-permute-start.5 = (f32[2,6,16,128]{3,2,1,0:T(8,128)S(1)}, f32[2,6,16,128]{3,2,1,0:T(8,128)S(1)}, u32[]{:S(2)}, u32[]{:S(2)}) collective-permute-start(f32[2,6,16,128]{3,2,1,0:T(8,128)S(1)} %get-tuple-element.7.own_ref), channel_id=1, source_target_pairs={{0,1},{2,3},{1,0},{3,2},{4,5},{6,7},{5,4},{7,6},{8,9},{10,11},{9,8... | collective-permute-start | bytes 294920 | tf_op jit(solution)/shard_map/ppermute | solution.py:316
  31.6 6.5 %collective-permute-start.6 = (f32[2,6,16,128]{3,2,1,0:T(8,128)S(1)}, f32[2,6,16,128]{3,2,1,0:T(8,128)S(1)}, u32[]{:S(2)}, u32[]{:S(2)}) collective-permute-start(f32[2,6,16,128]{3,2,1,0:T(8,128)S(1)} %get-tuple-element.7.own_ref), channel_id=1, source_target_pairs={{1,2},{2,1},{5,6},{6,5},{9,10},{10,9},{13,14},{14,13},{17,18},{18,... | collective-permute-start | bytes 294920 | tf_op jit(solution)/shard_map/ppermute | solution.py:316

commit v3 on v2

--- a/solution.py
+++ b/solution.py
@@ -194,17 +194,16 @@
 
 
 def filter_kernel(
-    odd_ref, near_ref, own_ref, far_ref, rows_ref, final_ref, fore_ref, back_ref,
+    high_ref, own_ref, low_ref, rows_ref, final_ref, fore_ref, back_ref,
     out_ref, field, spectra, weighted, result, fore, back,
 ):
     count = own_ref.shape[1]
-    odd = 32 * odd_ref[0]
     for p in range(count):
         lanes = pl.ds(128 * p, 128)
         for part in range(2):
-            for place, ref in ((32 - odd, near_ref), (16, own_ref), (odd, far_ref)):
+            for k, ref in enumerate((low_ref, own_ref, high_ref)):
                 high, low = split(ref[part, p])
-                at = pl.multiple_of(48 * part + place, 16)
+                at = 48 * part + 16 * k
                 field[pl.ds(at, 16), lanes] = high
                 field[pl.ds(96 + at, 16), lanes] = low
                 field[pl.ds(192 + at, 16), lanes] = high
@@ -278,14 +277,14 @@
             out_ref[part, p] = out[16 * part : 16 * part + 16, 128 * p : 128 * p + 128]
 
 
-def goldstein(odd, near, own, far):
+def goldstein(high, own, low):
     count = own.shape[1]
     vmem = pl.BlockSpec(memory_space=pltpu.VMEM)
     tables = [jnp.asarray(table) for table in filter_tables()]
     return pl.pallas_call(
         filter_kernel,
         out_shape=jax.ShapeDtypeStruct((2, count, 16, 128), F32),
-        in_specs=[pl.BlockSpec(memory_space=pltpu.SMEM)] + [vmem] * (3 + len(tables)),
+        in_specs=[vmem] * (3 + len(tables)),
         out_specs=vmem,
         scratch_shapes=[
             pltpu.VMEM((288, 128 * count), BF16),
@@ -297,7 +296,7 @@
         ],
         compiler_params=pltpu.CompilerParams(vmem_limit_bytes=16 << 20),
         name="goldstein",
-    )(odd, near, own, far, *tables)
+    )(high, own, low, *tables)
 
 
 def shifted(value, axis, step):
@@ -308,12 +307,6 @@
 def turned(value, axis, step):
     size = lax.axis_size(axis)
     return lax.ppermute(value, axis, [(i, (i + step) % size) for i in range(size)])
-
-
-def swapped(value, axis, first):
-    size = lax.axis_size(axis)
-    pairs = [(i, i + 1) for i in range(first, size - 1, 2)]
-    return lax.ppermute(value, axis, pairs + [(j, i) for i, j in pairs])
 
 
 COLUMNS = (1024, 512)
@@ -349,10 +342,10 @@
         here, own[-1], following[-1], int(ends[-2]), "looks_end",
         last=(is_last, own_last), extra=(*parts, returned),
     )
-    near = swapped(gamma, "space", 0)
-    far = swapped(gamma, "space", 1)
-    odd = (lax.axis_index("space") % 2).astype(jnp.int32).reshape(1)
-    return coherence, goldstein(odd, near, gamma, far)
+    strip, strips = lax.axis_index("space"), lax.axis_size("space")
+    low = jnp.where(strip == 0, 0.0, turned(gamma, "space", 1))
+    high = jnp.where(strip == strips - 1, 0.0, turned(gamma, "space", -1))
+    return coherence, goldstein(high, gamma, low)
 
 
 def solution(mesh):

time: 42 us -> 40.3 us (0.960)
  starting transfers between devices: 16.7 us -> 15.4 us
  waiting for transfers between devices: 11.7 us -> 11.1 us
    ppermute x2 -> x0, waiting for transfers between devices: 4.57 us -> none  [swapped(): return lax.ppermute(value, axis, pairs + [(j, i) for i, j in pairs])]
    ppermute x2 -> x4, waiting for transfers between devices: 6.28 us -> 10.3 us  [turned(): lax.ppermute(value, axis, [(i, (i + step) % size) for i in range(size)])]
    ppermute x2 -> x0, starting transfers between devices: 3.19 us -> none  [swapped(): return lax.ppermute(value, axis, pairs + [(j, i) for i, j in pairs])]
    ppermute x2 -> x4, starting transfers between devices: 7.57 us -> 9.6 us  [turned(): lax.ppermute(value, axis, [(i, (i + step) % size) for i in range(size)])]
  transfers between devices with their start and end apart: 7 -> 7, of which waited for: 5 -> 5; matrix products, arithmetic and copies ran while one was open for 1% -> 1% of each run, Pallas kernels for 11% -> 12%
where the time goes in v3:
time: 40.3 us; the launch traced here: 39.7 us
  starting transfers between devices  15.4 us (38%)
  waiting for transfers between devices  11.1 us (28%)
  Pallas kernels  10.7 us (27%)
  local copies, waits for them, and re-layouts  1.71 us (4%)
  between operations  0.78 us (2%)
    ppermute x4, waiting for transfers between devices, turned(): lax.ppermute(value, axis, [(i, (i + step) % size) for i in range(size)])  10.3 us
    ppermute x4, starting transfers between devices, turned(): lax.ppermute(value, axis, [(i, (i + step) % size) for i in range(size)])  9.6 us
    pallas_call x3, Pallas kernels, looks(): pl.pallas_call(functools.partial(looks_kernel, start=start, tables=len(ta...  7.31 us
    ppermute x3, starting transfers between devices, shifted(): lax.ppermute(value, axis, [(i, i + step) for i in range(size) if 0 <= i +...  5.79 us
    pallas_call x1, Pallas kernels, goldstein(): pl.pallas_call(filter_kernel, out_shape=jax.ShapeDtypeStruct((2, count, 1...  3.36 us
    slice x2, local copies, waits for them, and re-layouts, per_device(): own = [slc[..., at:at + width] for at, width in zip(ends, COLUMNS)]  1.59 us
    ppermute x3, waiting for transfers between devices, shifted(): lax.ppermute(value, axis, [(i, i + step) for i in range(size) if 0 <= i +...  0.81 us
  transfers between devices with their start and end apart: 7, of which 5 were waited for; matrix products, arithmetic and copies ran while one was open for 1% of the time, Pallas kernels for 12%

profile of v3, /device:TPU:16, one launch (start us, length us, event | category | flops | bytes accessed | tf_op | source)
XLA Modules:
  0.0 39.7 jit_solution(6803587998443488963)
XLA Ops:
  0.6 1.5 %slice.11.refs_1_ = bf16[2,4,64,1024]{3,2,1,0:T(8,128)(2,1)S(1)} slice(bf16[2,4,64,2048]{3,2,1,0:T(8,128)(2,1)} %param.6), slice={[0:2], [0:4], [0:64], [0:1024]} | slice | bytes 2097152 | tf_op jit(solution)/shard_map/slice | solution.py:325
  2.1 7.6 %collective-permute-start.3 = (bf16[2,4,64,1024]{3,2,1,0:T(8,128)(2,1)S(1)}, bf16[2,4,64,1024]{3,2,1,0:T(8,128)(2,1)S(1)}, u32[]{:S(2)}, u32[]{:S(2)}) collective-permute-start(bf16[2,4,64,1024]{3,2,1,0:T(8,128)(2,1)S(1)} %slice.11.refs_1_), channel_id=1, source_target_pairs={{0,252},{4,0},{8,4},{12,8},{16,12},{20,16},{24,20},{28,24},{32,28}... | collective-permute-start | bytes 3145736 | tf_op jit(solution)/shard_map/ppermute | solution.py:309
  9.7 0.1 fusion
  9.8 2.1 %collective-permute-start.1 = (bf16[2,4,64,512]{3,2,1,0:T(8,128)(2,1)S(1)}, bf16[2,4,64,512]{3,2,1,0:T(8,128)(2,1)}, u32[]{:S(2)}, u32[]{:S(2)}) collective-permute-start(bf16[2,4,64,512]{3,2,1,0:T(8,128)(2,1)S(1)} %get-tuple-element.9.refs_2_.refs_4_), channel_id=1, source_target_pairs={{0,4},{4,8},{8,12},{12,16},{16,20},{20,24},{24,28},{28,32},{32,36}... | collective-permute-start | bytes 1572872 | tf_op jit(solution)/shard_map/ppermute | solution.py:304
  11.9 0.0 collective-permute-start.2
  11.9 0.1 copy.8
  12.0 2.4 %collective-permute-start = (s32[6,2]{1,0:T(8,128)S(1)}, s32[6,2]{1,0:T(8,128)S(1)}, u32[]{:S(2)}, u32[]{:S(2)}) collective-permute-start(s32[6,2]{1,0:T(8,128)S(1)} %broadcast_subtract_fusion.refs_0_), channel_id=1, source_target_pairs={{0,4},{4,8},{8,12},{12,16},{16,20},{20,24},{24,28},{28,32},{32,36}... | collective-permute-start | bytes 152 | tf_op jit(solution)/shard_map/ppermute | solution.py:304
  14.4 0.8 %collective-permute-done = s32[6,2]{1,0:T(8,128)S(1)} collective-permute-done((s32[6,2]{1,0:T(8,128)S(1)}, s32[6,2]{1,0:T(8,128)S(1)}, u32[]{:S(2)}, u32[]{:S(2)}) %collective-permute-start) | collective-permute-done | bytes 80 | tf_op jit(solution)/shard_map/ppermute | solution.py:304
  15.2 0.0 collective-permute-done.1.refs_1_
  15.2 2.0 %looks_last.1 = f32[2,6,16,128]{3,2,1,0:T(8,128)S(1)} custom-call(s32[6,2]{1,0:T(8,128)S(1)} %broadcast_clamp_fusion.refs_0_, bf16[2,4,64,512]{3,2,1,0:T(8,128)(2,1)} %collective-permute-done.1.refs_1_, bf16[2,4,64,512]{3,2,1,0:T(8,128)(2,1)S(1)} %get-tuple-element.9.refs_2_.refs_4_), custom_call_target="tpu_custom_call" | custom-call | tf_op jit(solution)/shard_map/looks_last/pallas_call | solution.py:173
  17.3 1.3 %collective-permute-start.4 = (f32[2,6,16,128]{3,2,1,0:T(8,128)S(1)}, f32[2,6,16,128]{3,2,1,0:T(8,128)}, u32[]{:S(2)}, u32[]{:S(2)}) collective-permute-start(f32[2,6,16,128]{3,2,1,0:T(8,128)S(1)} %looks_last.1), channel_id=1, source_target_pairs={{4,0},{8,4},{12,8},{16,12},{20,16},{24,20},{28,24},{32,28},{36,32}... | collective-permute-start | bytes 294920 | tf_op jit(solution)/shard_map/ppermute | solution.py:304
  18.6 0.0 copy-start
  18.6 0.0 copy-start.1
  18.6 0.0 copy-start.2
  18.6 0.0 copy-start.3
  18.6 3.4 %collective-permute-done.3.refs_2_ = bf16[2,4,64,1024]{3,2,1,0:T(8,128)(2,1)S(1)} collective-permute-done((bf16[2,4,64,1024]{3,2,1,0:T(8,128)(2,1)S(1)}, bf16[2,4,64,1024]{3,2,1,0:T(8,128)(2,1)S(1)}, u32[]{:S(2)}, u32[]{:S(2)}) %collective-permute-start.3) | collective-permute-done | bytes 1048608 | tf_op jit(solution)/shard_map/ppermute | solution.py:309
  22.0 2.6 %looks_part.1.refs_5_ = f32[2,6,16,128]{3,2,1,0:T(8,128)S(1)} custom-call(s32[6,2]{1,0:T(8,128)S(1)} %broadcast_subtract_fusion.refs_0_, bf16[2,4,64,1024]{3,2,1,0:T(8,128)(2,1)S(1)} %slice.11.refs_1_, bf16[2,4,64,1024]{3,2,1,0:T(8,128)(2,1)S(1)} %collective-permute-done.3.refs_2_), custom_call_target="tpu_custom_call" | custom-call | tf_op jit(solution)/shard_map/looks_part/pallas_call | solution.py:173
  24.6 3.0 %collective-permute-done.2.refs_2_ = bf16[2,4,64,512]{3,2,1,0:T(8,128)(2,1)} collective-permute-done((bf16[2,4,64,512]{3,2,1,0:T(8,128)(2,1)S(1)}, bf16[2,4,64,512]{3,2,1,0:T(8,128)(2,1)}, u32[]{:S(2)}, u32[]{:S(2)}) %collective-permute-start.2) | collective-permute-done | bytes 524320 | tf_op jit(solution)/shard_map/ppermute | solution.py:309
  27.6 2.7 %looks_end.1 = (f32[2,6,16,128]{3,2,1,0:T(8,128)S(1)}, f32[6,16,128]{2,1,0:T(8,128)}) custom-call(s32[6,2]{1,0:T(8,128)S(1)} %broadcast_subtract_fusion.refs_0_, bf16[2,4,64,512]{3,2,1,0:T(8,128)(2,1)S(1)} %get-tuple-element.8.refs_1_, bf16[2,4,64,512]{3,2,1,0:T(8,128)(2,1)} %collective-permute-done.2.refs_2_, s32[1]{0:T(128)} %bitcast.refs_3_, ...), custom_call_target="tpu_custom_call" | custom-call | tf_op jit(solution)/shard_map/looks_end/pallas_call | solution.py:173
  30.3 1.3 %collective-permute-start.6 = (f32[2,6,16,128]{3,2,1,0:T(8,128)S(1)}, f32[2,6,16,128]{3,2,1,0:T(8,128)S(1)}, u32[]{:S(2)}, u32[]{:S(2)}) collective-permute-start(f32[2,6,16,128]{3,2,1,0:T(8,128)S(1)} %get-tuple-element.7.own_ref), channel_id=1, source_target_pairs={{0,1},{1,2},{2,3},{3,0},{4,5},{5,6},{6,7},{7,4},{8,9},{9,10},{10,1... | collective-permute-start | bytes 294920 | tf_op jit(solution)/shard_map/ppermute | solution.py:309
  31.6 0.7 %collective-permute-start.5 = (f32[2,6,16,128]{3,2,1,0:T(8,128)S(1)}, f32[2,6,16,128]{3,2,1,0:T(8,128)S(1)}, u32[]{:S(2)}, u32[]{:S(2)}) collective-permute-start(f32[2,6,16,128]{3,2,1,0:T(8,128)S(1)} %get-tuple-element.7.own_ref), channel_id=1, source_target_pairs={{0,3},{1,0},{2,1},{3,2},{4,7},{5,4},{6,5},{7,6},{8,11},{9,8},{10,9... | collective-permute-start | bytes 294920 | tf_op jit(solution)/shard_map/ppermute | solution.py:309
  32.4 2.6 %collective-permute-done.6 = f32[2,6,16,128]{3,2,1,0:T(8,128)S(1)} collective-permute-done((f32[2,6,16,128]{3,2,1,0:T(8,128)S(1)}, f32[2,6,16,128]{3,2,1,0:T(8,128)S(1)}, u32[]{:S(2)}, u32[]{:S(2)}) %collective-permute-start.6) | collective-permute-done | bytes 98336 | tf_op jit(solution)/shard_map/ppermute | solution.py:309
  35.0 1.3 %collective-permute-done.5 = f32[2,6,16,128]{3,2,1,0:T(8,128)S(1)} collective-permute-done((f32[2,6,16,128]{3,2,1,0:T(8,128)S(1)}, f32[2,6,16,128]{3,2,1,0:T(8,128)S(1)}, u32[]{:S(2)}, u32[]{:S(2)}) %collective-permute-start.5) | collective-permute-done | bytes 98336 | tf_op jit(solution)/shard_map/ppermute | solution.py:309
  36.3 3.4 %goldstein.1 = f32[2,6,16,128]{3,2,1,0:T(8,128)} custom-call(f32[2,6,16,128]{3,2,1,0:T(8,128)S(1)} %broadcast_select_fusion.1.high_ref, f32[2,6,16,128]{3,2,1,0:T(8,128)S(1)} %get-tuple-element.7.own_ref, f32[2,6,16,128]{3,2,1,0:T(8,128)S(1)} %broadcast_select_fusion.low_ref, bf16[128,288]{1,0:T(8,128)(2,1)S(1)} %copy-done.1, bf16[32,384]{1,0:T(8,128)(2,1)S(1)} %copy-done.3, ...), custom_call_target="tpu_custom_call" | custom-call | tf_op jit(solution)/shard_map/goldstein/pallas_call | solution.py:284
  (13 shorter events, 0.0 us)
Async XLA Ops:
  0.6 9.1 %copy-start.4 = (bf16[2,4,64,2048]{3,2,1,0:T(8,128)(2,1)S(1)}, bf16[2,4,64,2048]{3,2,1,0:T(8,128)(2,1)}, u32[]{:S(2)}) copy-start(bf16[2,4,64,2048]{3,2,1,0:T(8,128)(2,1)} %param.6) | copy-start | bytes 6291460
  0.6 11.3 %copy-start.5 = (s32[6,2]{0,1:T(2,128)S(1)}, s32[6,2]{0,1:T(2,128)}, u32[]{:S(2)}) copy-start(s32[6,2]{0,1:T(2,128)} %param.7) | copy-start | bytes 148
  2.1 19.9 %collective-permute-start.3 = (bf16[2,4,64,1024]{3,2,1,0:T(8,128)(2,1)S(1)}, bf16[2,4,64,1024]{3,2,1,0:T(8,128)(2,1)S(1)}, u32[]{:S(2)}, u32[]{:S(2)}) collective-permute-start(bf16[2,4,64,1024]{3,2,1,0:T(8,128)(2,1)S(1)} %slice.11.refs_1_), channel_id=1, source_target_pairs={{0,252},{4,0},{8,4},{12,8},{16,12},{20,16},{24,20},{28,24},{32,28}... | collective-permute-start | bytes 3145736 | tf_op jit(solution)/shard_map/ppermute | solution.py:309
  9.8 5.4 %collective-permute-start.1 = (bf16[2,4,64,512]{3,2,1,0:T(8,128)(2,1)S(1)}, bf16[2,4,64,512]{3,2,1,0:T(8,128)(2,1)}, u32[]{:S(2)}, u32[]{:S(2)}) collective-permute-start(bf16[2,4,64,512]{3,2,1,0:T(8,128)(2,1)S(1)} %get-tuple-element.9.refs_2_.refs_4_), channel_id=1, source_target_pairs={{0,4},{4,8},{8,12},{12,16},{16,20},{20,24},{24,28},{28,32},{32,36}... | collective-permute-start | bytes 1572872 | tf_op jit(solution)/shard_map/ppermute | solution.py:304
  11.9 15.7 %collective-permute-start.2 = (bf16[2,4,64,512]{3,2,1,0:T(8,128)(2,1)S(1)}, bf16[2,4,64,512]{3,2,1,0:T(8,128)(2,1)}, u32[]{:S(2)}, u32[]{:S(2)}) collective-permute-start(bf16[2,4,64,512]{3,2,1,0:T(8,128)(2,1)S(1)} %get-tuple-element.8.refs_1_), channel_id=1, source_target_pairs={{0,252},{4,0},{8,4},{12,8},{16,12},{20,16},{24,20},{28,24},{32,28}... | collective-permute-start | bytes 1572872 | tf_op jit(solution)/shard_map/ppermute | solution.py:309
  12.0 3.2 %collective-permute-start = (s32[6,2]{1,0:T(8,128)S(1)}, s32[6,2]{1,0:T(8,128)S(1)}, u32[]{:S(2)}, u32[]{:S(2)}) collective-permute-start(s32[6,2]{1,0:T(8,128)S(1)} %broadcast_subtract_fusion.refs_0_), channel_id=1, source_target_pairs={{0,4},{4,8},{8,12},{12,16},{16,20},{20,24},{24,28},{28,32},{32,36}... | collective-permute-start | bytes 152 | tf_op jit(solution)/shard_map/ppermute | solution.py:304
  17.3 10.4 %collective-permute-start.4 = (f32[2,6,16,128]{3,2,1,0:T(8,128)S(1)}, f32[2,6,16,128]{3,2,1,0:T(8,128)}, u32[]{:S(2)}, u32[]{:S(2)}) collective-permute-start(f32[2,6,16,128]{3,2,1,0:T(8,128)S(1)} %looks_last.1), channel_id=1, source_target_pairs={{4,0},{8,4},{12,8},{16,12},{20,16},{24,20},{28,24},{32,28},{36,32}... | collective-permute-start | bytes 294920 | tf_op jit(solution)/shard_map/ppermute | solution.py:304
  18.6 17.7 %copy-start = (bf16[4,128,128]{2,1,0:T(8,128)(2,1)S(1)}, bf16[4,128,128]{2,1,0:T(8,128)(2,1)}, u32[]{:S(2)}) copy-start(bf16[4,128,128]{2,1,0:T(8,128)(2,1)} %constant.32.clone.back_ref) | copy-start | bytes 393220
  18.6 17.7 %copy-start.1 = (bf16[128,288]{1,0:T(8,128)(2,1)S(1)}, bf16[128,288]{1,0:T(8,128)(2,1)}, u32[]{:S(2)}) copy-start(bf16[128,288]{1,0:T(8,128)(2,1)} %constant.29.clone.rows_ref) | copy-start | bytes 221188
  18.6 17.7 %copy-start.2 = (bf16[4,32,128]{2,1,0:T(8,128)(2,1)S(1)}, bf16[4,32,128]{2,1,0:T(8,128)(2,1)}, u32[]{:S(2)}) copy-start(bf16[4,32,128]{2,1,0:T(8,128)(2,1)} %constant.31.clone.fore_ref) | copy-start | bytes 98308
  18.6 17.7 %copy-start.3 = (bf16[32,384]{1,0:T(8,128)(2,1)S(1)}, bf16[32,384]{1,0:T(8,128)(2,1)}, u32[]{:S(2)}) copy-start(bf16[32,384]{1,0:T(8,128)(2,1)} %constant.30.clone.final_ref) | copy-start | bytes 73732
  30.3 4.6 %collective-permute-start.6 = (f32[2,6,16,128]{3,2,1,0:T(8,128)S(1)}, f32[2,6,16,128]{3,2,1,0:T(8,128)S(1)}, u32[]{:S(2)}, u32[]{:S(2)}) collective-permute-start(f32[2,6,16,128]{3,2,1,0:T(8,128)S(1)} %get-tuple-element.7.own_ref), channel_id=1, source_target_pairs={{0,1},{1,2},{2,3},{3,0},{4,5},{5,6},{6,7},{7,4},{8,9},{9,10},{10,1... | collective-permute-start | bytes 294920 | tf_op jit(solution)/shard_map/ppermute | solution.py:309
  31.6 4.6 %collective-permute-start.5 = (f32[2,6,16,128]{3,2,1,0:T(8,128)S(1)}, f32[2,6,16,128]{3,2,1,0:T(8,128)S(1)}, u32[]{:S(2)}, u32[]{:S(2)}) collective-permute-start(f32[2,6,16,128]{3,2,1,0:T(8,128)S(1)} %get-tuple-element.7.own_ref), channel_id=1, source_target_pairs={{0,3},{1,0},{2,1},{3,2},{4,7},{5,4},{6,5},{7,6},{8,11},{9,8},{10,9... | collective-permute-start | bytes 294920 | tf_op jit(solution)/shard_map/ppermute | solution.py:309

commit v4 on v3

--- a/solution.py
+++ b/solution.py
@@ -309,7 +309,7 @@
     return lax.ppermute(value, axis, [(i, (i + step) % size) for i in range(size)])
 
 
-COLUMNS = (1024, 512)
+COLUMNS = (1280, 256)
 
 
 def after(value, *done):

time: 40.3 us -> 40.2 us (level)
  local copies, waits for them, and re-layouts: 1.71 us -> 3.59 us
  waiting for transfers between devices: 11.1 us -> 9.36 us
  starting transfers between devices: 15.4 us -> 14.3 us
  Pallas kernels: 10.7 us -> 11.4 us
    ppermute x3, starting transfers between devices: 5.79 us -> 4.66 us  [shifted(): lax.ppermute(value, axis, [(i, i + step) for i in range(size) if 0 <= i +...]
    slice x0 -> x1, local copies, waits for them, and re-layouts: none -> 1.08 us  [per_device(): own_last = slc[..., edge:]]
    ppermute x4, waiting for transfers between devices: 10.3 us -> 9.35 us  [turned(): lax.ppermute(value, axis, [(i, (i + step) % size) for i in range(size)])]
    ppermute x3, waiting for transfers between devices: 0.81 us -> 0.01 us  [shifted(): lax.ppermute(value, axis, [(i, i + step) for i in range(size) if 0 <= i +...]
    slice x2, local copies, waits for them, and re-layouts: 1.59 us -> 2.38 us  [per_device(): own = [slc[..., at:at + width] for at, width in zip(ends, COLUMNS)]]
    pallas_call x3, Pallas kernels: 7.31 us -> 8.05 us  [looks(): pl.pallas_call(functools.partial(looks_kernel, start=start, tables=len(ta...]
  transfers between devices with their start and end apart: 7 -> 7, of which waited for: 5 -> 3; matrix products, arithmetic and copies ran while one was open for 1% -> 5% of each run, Pallas kernels for 12% -> 15%
where the time goes in v4:
time: 40.2 us; the launch traced here: 39.5 us
  starting transfers between devices  14.3 us (36%)
  Pallas kernels  11.4 us (28%)
  waiting for transfers between devices  9.36 us (23%)
  local copies, waits for them, and re-layouts  3.59 us (9%)
  between operations  0.8 us (2%)
    ppermute x4, starting transfers between devices, turned(): lax.ppermute(value, axis, [(i, (i + step) % size) for i in range(size)])  9.68 us
    ppermute x4, waiting for transfers between devices, turned(): lax.ppermute(value, axis, [(i, (i + step) % size) for i in range(size)])  9.35 us
    pallas_call x3, Pallas kernels, looks(): pl.pallas_call(functools.partial(looks_kernel, start=start, tables=len(ta...  8.05 us
    ppermute x3, starting transfers between devices, shifted(): lax.ppermute(value, axis, [(i, i + step) for i in range(size) if 0 <= i +...  4.66 us
    pallas_call x1, Pallas kernels, goldstein(): pl.pallas_call(filter_kernel, out_shape=jax.ShapeDtypeStruct((2, count, 1...  3.36 us
    slice x2, local copies, waits for them, and re-layouts, per_device(): own = [slc[..., at:at + width] for at, width in zip(ends, COLUMNS)]  2.38 us
    slice x1, local copies, waits for them, and re-layouts, per_device(): own_last = slc[..., edge:]  1.08 us
  transfers between devices with their start and end apart: 7, of which 3 were waited for; matrix products, arithmetic and copies ran while one was open for 5% of the time, Pallas kernels for 15%

profile of v4, /device:TPU:16, one launch (start us, length us, event | category | flops | bytes accessed | tf_op | source)
XLA Modules:
  0.0 39.5 jit_solution(4741672737220723563)
XLA Ops:
  0.6 1.4 %slice.11.refs_1_ = bf16[2,4,64,1280]{3,2,1,0:T(8,128)(2,1)S(1)} slice(bf16[2,4,64,2048]{3,2,1,0:T(8,128)(2,1)} %param.6), slice={[0:2], [0:4], [0:64], [0:1280]} | slice | bytes 2621440 | tf_op jit(solution)/shard_map/slice | solution.py:325
  2.0 7.6 %collective-permute-start.3 = (bf16[2,4,64,1280]{3,2,1,0:T(8,128)(2,1)S(1)}, bf16[2,4,64,1280]{3,2,1,0:T(8,128)(2,1)S(1)}, u32[]{:S(2)}, u32[]{:S(2)}) collective-permute-start(bf16[2,4,64,1280]{3,2,1,0:T(8,128)(2,1)S(1)} %slice.11.refs_1_), channel_id=1, source_target_pairs={{0,252},{4,0},{8,4},{12,8},{16,12},{20,16},{24,20},{28,24},{32,28}... | collective-permute-start | bytes 3932168 | tf_op jit(solution)/shard_map/ppermute | solution.py:309
  9.6 1.1 %slice.9.refs_2_.refs_4_ = bf16[2,4,64,512]{3,2,1,0:T(8,128)(2,1)S(1)} slice(bf16[2,4,64,2048]{3,2,1,0:T(8,128)(2,1)} %param.6), slice={[0:2], [0:4], [0:64], [1536:2048]} | slice | bytes 1048576 | tf_op jit(solution)/shard_map/slice | solution.py:326
  10.7 2.1 %collective-permute-start.1 = (bf16[2,4,64,512]{3,2,1,0:T(8,128)(2,1)S(1)}, bf16[2,4,64,512]{3,2,1,0:T(8,128)(2,1)}, u32[]{:S(2)}, u32[]{:S(2)}) collective-permute-start(bf16[2,4,64,512]{3,2,1,0:T(8,128)(2,1)S(1)} %slice.9.refs_2_.refs_4_), channel_id=1, source_target_pairs={{0,4},{4,8},{8,12},{12,16},{16,20},{20,24},{24,28},{28,32},{32,36}... | collective-permute-start | bytes 1572872 | tf_op jit(solution)/shard_map/ppermute | solution.py:304
  12.8 0.1 copy.8
  12.9 1.3 %collective-permute-start = (s32[6,2]{1,0:T(8,128)S(1)}, s32[6,2]{1,0:T(8,128)S(1)}, u32[]{:S(2)}, u32[]{:S(2)}) collective-permute-start(s32[6,2]{1,0:T(8,128)S(1)} %broadcast_subtract_fusion.refs_0_), channel_id=1, source_target_pairs={{0,4},{4,8},{8,12},{12,16},{16,20},{20,24},{24,28},{28,32},{32,36}... | collective-permute-start | bytes 152 | tf_op jit(solution)/shard_map/ppermute | solution.py:304
  14.2 1.0 %slice.10.refs_1_ = bf16[2,4,64,256]{3,2,1,0:T(8,128)(2,1)S(1)} slice(bf16[2,4,64,2048]{3,2,1,0:T(8,128)(2,1)} %param.6), slice={[0:2], [0:4], [0:64], [1280:1536]} | slice | bytes 524288 | tf_op jit(solution)/shard_map/slice | solution.py:325
  15.2 0.1 collective-permute-start.2
  15.3 2.7 %looks_last.1 = f32[2,6,16,128]{3,2,1,0:T(8,128)} custom-call(s32[6,2]{1,0:T(8,128)S(1)} %broadcast_clamp_fusion.refs_0_, bf16[2,4,64,512]{3,2,1,0:T(8,128)(2,1)} %collective-permute-done.1.refs_1_, bf16[2,4,64,512]{3,2,1,0:T(8,128)(2,1)S(1)} %slice.9.refs_2_.refs_4_), custom_call_target="tpu_custom_call" | custom-call | tf_op jit(solution)/shard_map/looks_last/pallas_call | solution.py:173
  18.0 1.3 %collective-permute-start.4 = (f32[2,6,16,128]{3,2,1,0:T(8,128)}, f32[2,6,16,128]{3,2,1,0:T(8,128)S(1)}, u32[]{:S(2)}, u32[]{:S(2)}) collective-permute-start(f32[2,6,16,128]{3,2,1,0:T(8,128)} %looks_last.1), channel_id=1, source_target_pairs={{4,0},{8,4},{12,8},{16,12},{20,16},{24,20},{28,24},{32,28},{36,32}... | collective-permute-start | bytes 294920 | tf_op jit(solution)/shard_map/ppermute | solution.py:304
  19.3 5.5 %collective-permute-done.3.refs_2_ = bf16[2,4,64,1280]{3,2,1,0:T(8,128)(2,1)S(1)} collective-permute-done((bf16[2,4,64,1280]{3,2,1,0:T(8,128)(2,1)S(1)}, bf16[2,4,64,1280]{3,2,1,0:T(8,128)(2,1)S(1)}, u32[]{:S(2)}, u32[]{:S(2)}) %collective-permute-start.3) | collective-permute-done | bytes 1310752 | tf_op jit(solution)/shard_map/ppermute | solution.py:309
  24.7 3.2 %looks_part.1.refs_5_ = f32[2,6,16,128]{3,2,1,0:T(8,128)S(1)} custom-call(s32[6,2]{1,0:T(8,128)S(1)} %broadcast_subtract_fusion.refs_0_, bf16[2,4,64,1280]{3,2,1,0:T(8,128)(2,1)S(1)} %slice.11.refs_1_, bf16[2,4,64,1280]{3,2,1,0:T(8,128)(2,1)S(1)} %collective-permute-done.3.refs_2_), custom_call_target="tpu_custom_call" | custom-call | tf_op jit(solution)/shard_map/looks_part/pallas_call | solution.py:173
  27.9 0.0 copy-start
  27.9 0.0 copy-start.1
  28.0 0.0 copy-start.2
  28.0 0.0 copy-start.3
  28.0 0.0 collective-permute-done.2.refs_2_
  28.0 0.0 collective-permute-done.4.refs_6_
  28.0 2.2 %looks_end.1 = (f32[2,6,16,128]{3,2,1,0:T(8,128)S(1)}, f32[6,16,128]{2,1,0:T(8,128)}) custom-call(s32[6,2]{1,0:T(8,128)S(1)} %broadcast_subtract_fusion.refs_0_, bf16[2,4,64,256]{3,2,1,0:T(8,128)(2,1)S(1)} %slice.10.refs_1_, bf16[2,4,64,256]{3,2,1,0:T(8,128)(2,1)} %collective-permute-done.2.refs_2_, s32[1]{0:T(128)} %bitcast.refs_3_, ...), custom_call_target="tpu_custom_call" | custom-call | tf_op jit(solution)/shard_map/looks_end/pallas_call | solution.py:173
  30.2 1.3 %collective-permute-start.6 = (f32[2,6,16,128]{3,2,1,0:T(8,128)S(1)}, f32[2,6,16,128]{3,2,1,0:T(8,128)S(1)}, u32[]{:S(2)}, u32[]{:S(2)}) collective-permute-start(f32[2,6,16,128]{3,2,1,0:T(8,128)S(1)} %get-tuple-element.7.own_ref), channel_id=1, source_target_pairs={{0,1},{1,2},{2,3},{3,0},{4,5},{5,6},{6,7},{7,4},{8,9},{9,10},{10,1... | collective-permute-start | bytes 294920 | tf_op jit(solution)/shard_map/ppermute | solution.py:309
  31.5 0.7 %collective-permute-start.5 = (f32[2,6,16,128]{3,2,1,0:T(8,128)S(1)}, f32[2,6,16,128]{3,2,1,0:T(8,128)S(1)}, u32[]{:S(2)}, u32[]{:S(2)}) collective-permute-start(f32[2,6,16,128]{3,2,1,0:T(8,128)S(1)} %get-tuple-element.7.own_ref), channel_id=1, source_target_pairs={{0,3},{1,0},{2,1},{3,2},{4,7},{5,4},{6,5},{7,6},{8,11},{9,8},{10,9... | collective-permute-start | bytes 294920 | tf_op jit(solution)/shard_map/ppermute | solution.py:309
  32.2 2.6 %collective-permute-done.6 = f32[2,6,16,128]{3,2,1,0:T(8,128)S(1)} collective-permute-done((f32[2,6,16,128]{3,2,1,0:T(8,128)S(1)}, f32[2,6,16,128]{3,2,1,0:T(8,128)S(1)}, u32[]{:S(2)}, u32[]{:S(2)}) %collective-permute-start.6) | collective-permute-done | bytes 98336 | tf_op jit(solution)/shard_map/ppermute | solution.py:309
  34.8 1.3 %collective-permute-done.5 = f32[2,6,16,128]{3,2,1,0:T(8,128)S(1)} collective-permute-done((f32[2,6,16,128]{3,2,1,0:T(8,128)S(1)}, f32[2,6,16,128]{3,2,1,0:T(8,128)S(1)}, u32[]{:S(2)}, u32[]{:S(2)}) %collective-permute-start.5) | collective-permute-done | bytes 98336 | tf_op jit(solution)/shard_map/ppermute | solution.py:309
  36.2 3.4 %goldstein.1 = f32[2,6,16,128]{3,2,1,0:T(8,128)} custom-call(f32[2,6,16,128]{3,2,1,0:T(8,128)S(1)} %broadcast_select_fusion.1.high_ref, f32[2,6,16,128]{3,2,1,0:T(8,128)S(1)} %get-tuple-element.7.own_ref, f32[2,6,16,128]{3,2,1,0:T(8,128)S(1)} %broadcast_select_fusion.low_ref, bf16[128,288]{1,0:T(8,128)(2,1)S(1)} %copy-done.1, bf16[32,384]{1,0:T(8,128)(2,1)S(1)} %copy-done.3, ...), custom_call_target="tpu_custom_call" | custom-call | tf_op jit(solution)/shard_map/goldstein/pallas_call | solution.py:284
  (12 shorter events, 0.0 us)
Async XLA Ops:
  0.6 12.2 %copy-start.4 = (s32[6,2]{0,1:T(2,128)S(1)}, s32[6,2]{0,1:T(2,128)}, u32[]{:S(2)}) copy-start(s32[6,2]{0,1:T(2,128)} %param.7) | copy-start | bytes 148
  2.0 22.7 %collective-permute-start.3 = (bf16[2,4,64,1280]{3,2,1,0:T(8,128)(2,1)S(1)}, bf16[2,4,64,1280]{3,2,1,0:T(8,128)(2,1)S(1)}, u32[]{:S(2)}, u32[]{:S(2)}) collective-permute-start(bf16[2,4,64,1280]{3,2,1,0:T(8,128)(2,1)S(1)} %slice.11.refs_1_), channel_id=1, source_target_pairs={{0,252},{4,0},{8,4},{12,8},{16,12},{20,16},{24,20},{28,24},{32,28}... | collective-permute-start | bytes 3932168 | tf_op jit(solution)/shard_map/ppermute | solution.py:309
  10.7 4.6 %collective-permute-start.1 = (bf16[2,4,64,512]{3,2,1,0:T(8,128)(2,1)S(1)}, bf16[2,4,64,512]{3,2,1,0:T(8,128)(2,1)}, u32[]{:S(2)}, u32[]{:S(2)}) collective-permute-start(bf16[2,4,64,512]{3,2,1,0:T(8,128)(2,1)S(1)} %slice.9.refs_2_.refs_4_), channel_id=1, source_target_pairs={{0,4},{4,8},{8,12},{12,16},{16,20},{20,24},{24,28},{28,32},{32,36}... | collective-permute-start | bytes 1572872 | tf_op jit(solution)/shard_map/ppermute | solution.py:304
  12.9 2.4 %collective-permute-start = (s32[6,2]{1,0:T(8,128)S(1)}, s32[6,2]{1,0:T(8,128)S(1)}, u32[]{:S(2)}, u32[]{:S(2)}) collective-permute-start(s32[6,2]{1,0:T(8,128)S(1)} %broadcast_subtract_fusion.refs_0_), channel_id=1, source_target_pairs={{0,4},{4,8},{8,12},{12,16},{16,20},{20,24},{24,28},{28,32},{32,36}... | collective-permute-start | bytes 152 | tf_op jit(solution)/shard_map/ppermute | solution.py:304
  15.2 12.8 %collective-permute-start.2 = (bf16[2,4,64,256]{3,2,1,0:T(8,128)(2,1)S(1)}, bf16[2,4,64,256]{3,2,1,0:T(8,128)(2,1)}, u32[]{:S(2)}, u32[]{:S(2)}) collective-permute-start(bf16[2,4,64,256]{3,2,1,0:T(8,128)(2,1)S(1)} %slice.10.refs_1_), channel_id=1, source_target_pairs={{0,252},{4,0},{8,4},{12,8},{16,12},{20,16},{24,20},{28,24},{32,28}... | collective-permute-start | bytes 786440 | tf_op jit(solution)/shard_map/ppermute | solution.py:309
  18.0 10.0 %collective-permute-start.4 = (f32[2,6,16,128]{3,2,1,0:T(8,128)}, f32[2,6,16,128]{3,2,1,0:T(8,128)S(1)}, u32[]{:S(2)}, u32[]{:S(2)}) collective-permute-start(f32[2,6,16,128]{3,2,1,0:T(8,128)} %looks_last.1), channel_id=1, source_target_pairs={{4,0},{8,4},{12,8},{16,12},{20,16},{24,20},{28,24},{32,28},{36,32}... | collective-permute-start | bytes 294920 | tf_op jit(solution)/shard_map/ppermute | solution.py:304
  27.9 8.2 %copy-start = (bf16[4,128,128]{2,1,0:T(8,128)(2,1)S(1)}, bf16[4,128,128]{2,1,0:T(8,128)(2,1)}, u32[]{:S(2)}) copy-start(bf16[4,128,128]{2,1,0:T(8,128)(2,1)} %constant.32.clone.back_ref) | copy-start | bytes 393220
  27.9 8.2 %copy-start.1 = (bf16[128,288]{1,0:T(8,128)(2,1)S(1)}, bf16[128,288]{1,0:T(8,128)(2,1)}, u32[]{:S(2)}) copy-start(bf16[128,288]{1,0:T(8,128)(2,1)} %constant.29.clone.rows_ref) | copy-start | bytes 221188
  28.0 8.2 %copy-start.2 = (bf16[4,32,128]{2,1,0:T(8,128)(2,1)S(1)}, bf16[4,32,128]{2,1,0:T(8,128)(2,1)}, u32[]{:S(2)}) copy-start(bf16[4,32,128]{2,1,0:T(8,128)(2,1)} %constant.31.clone.fore_ref) | copy-start | bytes 98308
  28.0 8.2 %copy-start.3 = (bf16[32,384]{1,0:T(8,128)(2,1)S(1)}, bf16[32,384]{1,0:T(8,128)(2,1)}, u32[]{:S(2)}) copy-start(bf16[32,384]{1,0:T(8,128)(2,1)} %constant.30.clone.final_ref) | copy-start | bytes 73732
  30.2 4.6 %collective-permute-start.6 = (f32[2,6,16,128]{3,2,1,0:T(8,128)S(1)}, f32[2,6,16,128]{3,2,1,0:T(8,128)S(1)}, u32[]{:S(2)}, u32[]{:S(2)}) collective-permute-start(f32[2,6,16,128]{3,2,1,0:T(8,128)S(1)} %get-tuple-element.7.own_ref), channel_id=1, source_target_pairs={{0,1},{1,2},{2,3},{3,0},{4,5},{5,6},{6,7},{7,4},{8,9},{9,10},{10,1... | collective-permute-start | bytes 294920 | tf_op jit(solution)/shard_map/ppermute | solution.py:309
  31.5 4.6 %collective-permute-start.5 = (f32[2,6,16,128]{3,2,1,0:T(8,128)S(1)}, f32[2,6,16,128]{3,2,1,0:T(8,128)S(1)}, u32[]{:S(2)}, u32[]{:S(2)}) collective-permute-start(f32[2,6,16,128]{3,2,1,0:T(8,128)S(1)} %get-tuple-element.7.own_ref), channel_id=1, source_target_pairs={{0,3},{1,0},{2,1},{3,2},{4,7},{5,4},{6,5},{7,6},{8,11},{9,8},{10,9... | collective-permute-start | bytes 294920 | tf_op jit(solution)/shard_map/ppermute | solution.py:309

commit v5 on v4

--- a/solution.py
+++ b/solution.py
@@ -309,7 +309,7 @@
     return lax.ppermute(value, axis, [(i, (i + step) % size) for i in range(size)])
 
 
-COLUMNS = (1280, 256)
+COLUMNS = (768, 768)
 
 
 def after(value, *done):

time: 40.2 us -> 40.3 us (level)
  waiting for transfers between devices: 9.36 us -> 10.7 us
  Pallas kernels: 11.4 us -> 10.3 us
  local copies, waits for them, and re-layouts: 3.59 us -> 2.69 us
  starting transfers between devices: 14.3 us -> 15.2 us
    ppermute x3, waiting for transfers between devices: 0.01 us -> 2.62 us  [shifted(): lax.ppermute(value, axis, [(i, i + step) for i in range(size) if 0 <= i +...]
    ppermute x4, waiting for transfers between devices: 9.35 us -> 8.06 us  [turned(): lax.ppermute(value, axis, [(i, (i + step) % size) for i in range(size)])]
    pallas_call x3, Pallas kernels: 8.05 us -> 6.94 us  [looks(): pl.pallas_call(functools.partial(looks_kernel, start=start, tables=len(ta...]
    slice x2 -> x1, local copies, waits for them, and re-layouts: 2.38 us -> 1.49 us  [per_device(): own = [slc[..., at:at + width] for at, width in zip(ends, COLUMNS)]]
    ppermute x4, starting transfers between devices: 9.68 us -> 10.3 us  [turned(): lax.ppermute(value, axis, [(i, (i + step) % size) for i in range(size)])]
  transfers between devices with their start and end apart: 7 -> 7, of which waited for: 3 -> 6; matrix products, arithmetic and copies ran while one was open for 5% -> 3% of each run, Pallas kernels for 15% -> 11%
where the time goes in v5:
time: 40.3 us; the launch traced here: 39.7 us
  starting transfers between devices  15.2 us (38%)
  waiting for transfers between devices  10.7 us (27%)
  Pallas kernels  10.3 us (26%)
  local copies, waits for them, and re-layouts  2.69 us (7%)
  between operations  0.79 us (2%)
    ppermute x4, starting transfers between devices, turned(): lax.ppermute(value, axis, [(i, (i + step) % size) for i in range(size)])  10.3 us
    ppermute x4, waiting for transfers between devices, turned(): lax.ppermute(value, axis, [(i, (i + step) % size) for i in range(size)])  8.06 us
    pallas_call x3, Pallas kernels, looks(): pl.pallas_call(functools.partial(looks_kernel, start=start, tables=len(ta...  6.94 us
    ppermute x3, starting transfers between devices, shifted(): lax.ppermute(value, axis, [(i, i + step) for i in range(size) if 0 <= i +...  4.94 us
    pallas_call x1, Pallas kernels, goldstein(): pl.pallas_call(filter_kernel, out_shape=jax.ShapeDtypeStruct((2, count, 1...  3.35 us
    ppermute x3, waiting for transfers between devices, shifted(): lax.ppermute(value, axis, [(i, i + step) for i in range(size) if 0 <= i +...  2.62 us
    slice x1, local copies, waits for them, and re-layouts, per_device(): own = [slc[..., at:at + width] for at, width in zip(ends, COLUMNS)]  1.49 us
    slice x1, local copies, waits for them, and re-layouts, per_device(): own_last = slc[..., edge:]  1.08 us
  transfers between devices with their start and end apart: 7, of which 6 were waited for; matrix products, arithmetic and copies ran while one was open for 3% of the time, Pallas kernels for 11%

profile of v5, /device:TPU:16, one launch (start us, length us, event | category | flops | bytes accessed | tf_op | source)
XLA Modules:
  0.0 39.7 jit_solution(15644211984318145770)
XLA Ops:
  0.6 1.5 %fusion = (bf16[2,4,64,768]{3,2,1,0:T(8,128)(2,1)S(1)}, bf16[2,4,64,768]{3,2,1,0:T(8,128)(2,1)S(1)}) fusion(bf16[2,4,64,2048]{3,2,1,0:T(8,128)(2,1)} %param.6), kind=kLoop, calls=%fused_computation.4 | loop fusion | bytes 3145728 | tf_op jit(solution)/shard_map/slice | solution.py:325
  2.1 7.6 %collective-permute-start.3 = (bf16[2,4,64,768]{3,2,1,0:T(8,128)(2,1)S(1)}, bf16[2,4,64,768]{3,2,1,0:T(8,128)(2,1)}, u32[]{:S(2)}, u32[]{:S(2)}) collective-permute-start(bf16[2,4,64,768]{3,2,1,0:T(8,128)(2,1)S(1)} %get-tuple-element.8.refs_1_), channel_id=1, source_target_pairs={{0,252},{4,0},{8,4},{12,8},{16,12},{20,16},{24,20},{28,24},{32,28}... | collective-permute-start | bytes 2359304 | tf_op jit(solution)/shard_map/ppermute | solution.py:309
  9.7 0.7 %collective-permute-start.2 = (bf16[2,4,64,768]{3,2,1,0:T(8,128)(2,1)S(1)}, bf16[2,4,64,768]{3,2,1,0:T(8,128)(2,1)S(1)}, u32[]{:S(2)}, u32[]{:S(2)}) collective-permute-start(bf16[2,4,64,768]{3,2,1,0:T(8,128)(2,1)S(1)} %get-tuple-element.9.refs_1_), channel_id=1, source_target_pairs={{0,252},{4,0},{8,4},{12,8},{16,12},{20,16},{24,20},{28,24},{32,28}... | collective-permute-start | bytes 2359304 | tf_op jit(solution)/shard_map/ppermute | solution.py:309
  10.4 1.1 %slice.9.refs_2_.refs_4_ = bf16[2,4,64,512]{3,2,1,0:T(8,128)(2,1)S(1)} slice(bf16[2,4,64,2048]{3,2,1,0:T(8,128)(2,1)} %param.6), slice={[0:2], [0:4], [0:64], [1536:2048]} | slice | bytes 1048576 | tf_op jit(solution)/shard_map/slice | solution.py:326
  11.5 1.8 %collective-permute-start.1 = (bf16[2,4,64,512]{3,2,1,0:T(8,128)(2,1)S(1)}, bf16[2,4,64,512]{3,2,1,0:T(8,128)(2,1)S(1)}, u32[]{:S(2)}, u32[]{:S(2)}) collective-permute-start(bf16[2,4,64,512]{3,2,1,0:T(8,128)(2,1)S(1)} %slice.9.refs_2_.refs_4_), channel_id=1, source_target_pairs={{0,4},{4,8},{8,12},{12,16},{16,20},{20,24},{24,28},{28,32},{32,36}... | collective-permute-start | bytes 1572872 | tf_op jit(solution)/shard_map/ppermute | solution.py:304
  13.3 0.1 copy.8
  13.4 1.9 %collective-permute-start = (s32[6,2]{1,0:T(8,128)S(1)}, s32[6,2]{1,0:T(8,128)S(1)}, u32[]{:S(2)}, u32[]{:S(2)}) collective-permute-start(s32[6,2]{1,0:T(8,128)S(1)} %broadcast_subtract_fusion.refs_0_), channel_id=1, source_target_pairs={{0,4},{4,8},{8,12},{12,16},{16,20},{20,24},{24,28},{28,32},{32,36}... | collective-permute-start | bytes 152 | tf_op jit(solution)/shard_map/ppermute | solution.py:304
  15.2 0.8 %collective-permute-done = s32[6,2]{1,0:T(8,128)S(1)} collective-permute-done((s32[6,2]{1,0:T(8,128)S(1)}, s32[6,2]{1,0:T(8,128)S(1)}, u32[]{:S(2)}, u32[]{:S(2)}) %collective-permute-start) | collective-permute-done | bytes 80 | tf_op jit(solution)/shard_map/ppermute | solution.py:304
  16.1 1.6 %looks_last.1 = f32[2,6,16,128]{3,2,1,0:T(8,128)S(1)} custom-call(s32[6,2]{1,0:T(8,128)S(1)} %broadcast_clamp_fusion.refs_0_, bf16[2,4,64,512]{3,2,1,0:T(8,128)(2,1)S(1)} %collective-permute-done.1.refs_1_, bf16[2,4,64,512]{3,2,1,0:T(8,128)(2,1)S(1)} %slice.9.refs_2_.refs_4_), custom_call_target="tpu_custom_call" | custom-call | tf_op jit(solution)/shard_map/looks_last/pallas_call | solution.py:173
  17.6 1.3 %collective-permute-start.4 = (f32[2,6,16,128]{3,2,1,0:T(8,128)S(1)}, f32[2,6,16,128]{3,2,1,0:T(8,128)S(1)}, u32[]{:S(2)}, u32[]{:S(2)}) collective-permute-start(f32[2,6,16,128]{3,2,1,0:T(8,128)S(1)} %looks_last.1), channel_id=1, source_target_pairs={{4,0},{8,4},{12,8},{16,12},{20,16},{24,20},{28,24},{32,28},{36,32}... | collective-permute-start | bytes 294920 | tf_op jit(solution)/shard_map/ppermute | solution.py:304
  18.9 0.0 copy-start
  18.9 0.0 copy-start.1
  19.0 0.0 copy-start.2
  19.0 0.0 copy-start.3
  19.0 0.2 collective-permute-done.3.refs_2_
  19.2 2.6 %looks_part.1.refs_5_ = f32[2,6,16,128]{3,2,1,0:T(8,128)S(1)} custom-call(s32[6,2]{1,0:T(8,128)S(1)} %broadcast_subtract_fusion.refs_0_, bf16[2,4,64,768]{3,2,1,0:T(8,128)(2,1)S(1)} %get-tuple-element.8.refs_1_, bf16[2,4,64,768]{3,2,1,0:T(8,128)(2,1)} %collective-permute-done.3.refs_2_), custom_call_target="tpu_custom_call" | custom-call | tf_op jit(solution)/shard_map/looks_part/pallas_call | solution.py:173
  21.8 1.8 %collective-permute-done.4.refs_6_ = f32[2,6,16,128]{3,2,1,0:T(8,128)S(1)} collective-permute-done((f32[2,6,16,128]{3,2,1,0:T(8,128)S(1)}, f32[2,6,16,128]{3,2,1,0:T(8,128)S(1)}, u32[]{:S(2)}, u32[]{:S(2)}) %collective-permute-start.4) | collective-permute-done | bytes 98336 | tf_op jit(solution)/shard_map/ppermute | solution.py:304
  23.7 4.0 %collective-permute-done.2.refs_2_ = bf16[2,4,64,768]{3,2,1,0:T(8,128)(2,1)S(1)} collective-permute-done((bf16[2,4,64,768]{3,2,1,0:T(8,128)(2,1)S(1)}, bf16[2,4,64,768]{3,2,1,0:T(8,128)(2,1)S(1)}, u32[]{:S(2)}, u32[]{:S(2)}) %collective-permute-start.2) | collective-permute-done | bytes 786464 | tf_op jit(solution)/shard_map/ppermute | solution.py:309
  27.6 2.7 %looks_end.1 = (f32[2,6,16,128]{3,2,1,0:T(8,128)S(1)}, f32[6,16,128]{2,1,0:T(8,128)}) custom-call(s32[6,2]{1,0:T(8,128)S(1)} %broadcast_subtract_fusion.refs_0_, bf16[2,4,64,768]{3,2,1,0:T(8,128)(2,1)S(1)} %get-tuple-element.9.refs_1_, bf16[2,4,64,768]{3,2,1,0:T(8,128)(2,1)S(1)} %collective-permute-done.2.refs_2_, s32[1]{0:T(128)} %bitcast.refs_3_, ...), custom_call_target="tpu_custom_call" | custom-call | tf_op jit(solution)/shard_map/looks_end/pallas_call | solution.py:173
  30.4 1.3 %collective-permute-start.6 = (f32[2,6,16,128]{3,2,1,0:T(8,128)S(1)}, f32[2,6,16,128]{3,2,1,0:T(8,128)S(1)}, u32[]{:S(2)}, u32[]{:S(2)}) collective-permute-start(f32[2,6,16,128]{3,2,1,0:T(8,128)S(1)} %get-tuple-element.7.own_ref), channel_id=1, source_target_pairs={{0,1},{1,2},{2,3},{3,0},{4,5},{5,6},{6,7},{7,4},{8,9},{9,10},{10,1... | collective-permute-start | bytes 294920 | tf_op jit(solution)/shard_map/ppermute | solution.py:309
  31.7 0.7 %collective-permute-start.5 = (f32[2,6,16,128]{3,2,1,0:T(8,128)S(1)}, f32[2,6,16,128]{3,2,1,0:T(8,128)S(1)}, u32[]{:S(2)}, u32[]{:S(2)}) collective-permute-start(f32[2,6,16,128]{3,2,1,0:T(8,128)S(1)} %get-tuple-element.7.own_ref), channel_id=1, source_target_pairs={{0,3},{1,0},{2,1},{3,2},{4,7},{5,4},{6,5},{7,6},{8,11},{9,8},{10,9... | collective-permute-start | bytes 294920 | tf_op jit(solution)/shard_map/ppermute | solution.py:309
  32.4 2.7 %collective-permute-done.6 = f32[2,6,16,128]{3,2,1,0:T(8,128)S(1)} collective-permute-done((f32[2,6,16,128]{3,2,1,0:T(8,128)S(1)}, f32[2,6,16,128]{3,2,1,0:T(8,128)S(1)}, u32[]{:S(2)}, u32[]{:S(2)}) %collective-permute-start.6) | collective-permute-done | bytes 98336 | tf_op jit(solution)/shard_map/ppermute | solution.py:309
  35.1 1.2 %collective-permute-done.5 = f32[2,6,16,128]{3,2,1,0:T(8,128)S(1)} collective-permute-done((f32[2,6,16,128]{3,2,1,0:T(8,128)S(1)}, f32[2,6,16,128]{3,2,1,0:T(8,128)S(1)}, u32[]{:S(2)}, u32[]{:S(2)}) %collective-permute-start.5) | collective-permute-done | bytes 98336 | tf_op jit(solution)/shard_map/ppermute | solution.py:309
  36.3 3.4 %goldstein.1 = f32[2,6,16,128]{3,2,1,0:T(8,128)} custom-call(f32[2,6,16,128]{3,2,1,0:T(8,128)S(1)} %broadcast_select_fusion.1.high_ref, f32[2,6,16,128]{3,2,1,0:T(8,128)S(1)} %get-tuple-element.7.own_ref, f32[2,6,16,128]{3,2,1,0:T(8,128)S(1)} %broadcast_select_fusion.low_ref, bf16[128,288]{1,0:T(8,128)(2,1)S(1)} %copy-done.1, bf16[32,384]{1,0:T(8,128)(2,1)S(1)} %copy-done.3, ...), custom_call_target="tpu_custom_call" | custom-call | tf_op jit(solution)/shard_map/goldstein/pallas_call | solution.py:284
  (11 shorter events, 0.0 us)
Async XLA Ops:
  0.6 12.6 %copy-start.4 = (s32[6,2]{0,1:T(2,128)S(1)}, s32[6,2]{0,1:T(2,128)}, u32[]{:S(2)}) copy-start(s32[6,2]{0,1:T(2,128)} %param.7) | copy-start | bytes 148
  2.1 17.1 %collective-permute-start.3 = (bf16[2,4,64,768]{3,2,1,0:T(8,128)(2,1)S(1)}, bf16[2,4,64,768]{3,2,1,0:T(8,128)(2,1)}, u32[]{:S(2)}, u32[]{:S(2)}) collective-permute-start(bf16[2,4,64,768]{3,2,1,0:T(8,128)(2,1)S(1)} %get-tuple-element.8.refs_1_), channel_id=1, source_target_pairs={{0,252},{4,0},{8,4},{12,8},{16,12},{20,16},{24,20},{28,24},{32,28}... | collective-permute-start | bytes 2359304 | tf_op jit(solution)/shard_map/ppermute | solution.py:309
  9.7 17.9 %collective-permute-start.2 = (bf16[2,4,64,768]{3,2,1,0:T(8,128)(2,1)S(1)}, bf16[2,4,64,768]{3,2,1,0:T(8,128)(2,1)S(1)}, u32[]{:S(2)}, u32[]{:S(2)}) collective-permute-start(bf16[2,4,64,768]{3,2,1,0:T(8,128)(2,1)S(1)} %get-tuple-element.9.refs_1_), channel_id=1, source_target_pairs={{0,252},{4,0},{8,4},{12,8},{16,12},{20,16},{24,20},{28,24},{32,28}... | collective-permute-start | bytes 2359304 | tf_op jit(solution)/shard_map/ppermute | solution.py:309
  11.5 4.6 %collective-permute-start.1 = (bf16[2,4,64,512]{3,2,1,0:T(8,128)(2,1)S(1)}, bf16[2,4,64,512]{3,2,1,0:T(8,128)(2,1)S(1)}, u32[]{:S(2)}, u32[]{:S(2)}) collective-permute-start(bf16[2,4,64,512]{3,2,1,0:T(8,128)(2,1)S(1)} %slice.9.refs_2_.refs_4_), channel_id=1, source_target_pairs={{0,4},{4,8},{8,12},{12,16},{16,20},{20,24},{24,28},{28,32},{32,36}... | collective-permute-start | bytes 1572872 | tf_op jit(solution)/shard_map/ppermute | solution.py:304
  13.4 2.7 %collective-permute-start = (s32[6,2]{1,0:T(8,128)S(1)}, s32[6,2]{1,0:T(8,128)S(1)}, u32[]{:S(2)}, u32[]{:S(2)}) collective-permute-start(s32[6,2]{1,0:T(8,128)S(1)} %broadcast_subtract_fusion.refs_0_), channel_id=1, source_target_pairs={{0,4},{4,8},{8,12},{12,16},{16,20},{20,24},{24,28},{28,32},{32,36}... | collective-permute-start | bytes 152 | tf_op jit(solution)/shard_map/ppermute | solution.py:304
  17.6 6.0 %collective-permute-start.4 = (f32[2,6,16,128]{3,2,1,0:T(8,128)S(1)}, f32[2,6,16,128]{3,2,1,0:T(8,128)S(1)}, u32[]{:S(2)}, u32[]{:S(2)}) collective-permute-start(f32[2,6,16,128]{3,2,1,0:T(8,128)S(1)} %looks_last.1), channel_id=1, source_target_pairs={{4,0},{8,4},{12,8},{16,12},{20,16},{24,20},{28,24},{32,28},{36,32}... | collective-permute-start | bytes 294920 | tf_op jit(solution)/shard_map/ppermute | solution.py:304
  18.9 17.4 %copy-start = (bf16[4,128,128]{2,1,0:T(8,128)(2,1)S(1)}, bf16[4,128,128]{2,1,0:T(8,128)(2,1)}, u32[]{:S(2)}) copy-start(bf16[4,128,128]{2,1,0:T(8,128)(2,1)} %constant.32.clone.back_ref) | copy-start | bytes 393220
  18.9 17.4 %copy-start.1 = (bf16[128,288]{1,0:T(8,128)(2,1)S(1)}, bf16[128,288]{1,0:T(8,128)(2,1)}, u32[]{:S(2)}) copy-start(bf16[128,288]{1,0:T(8,128)(2,1)} %constant.29.clone.rows_ref) | copy-start | bytes 221188
  19.0 17.4 %copy-start.2 = (bf16[4,32,128]{2,1,0:T(8,128)(2,1)S(1)}, bf16[4,32,128]{2,1,0:T(8,128)(2,1)}, u32[]{:S(2)}) copy-start(bf16[4,32,128]{2,1,0:T(8,128)(2,1)} %constant.31.clone.fore_ref) | copy-start | bytes 98308
  19.0 17.4 %copy-start.3 = (bf16[32,384]{1,0:T(8,128)(2,1)S(1)}, bf16[32,384]{1,0:T(8,128)(2,1)}, u32[]{:S(2)}) copy-start(bf16[32,384]{1,0:T(8,128)(2,1)} %constant.30.clone.final_ref) | copy-start | bytes 73732
  30.4 4.7 %collective-permute-start.6 = (f32[2,6,16,128]{3,2,1,0:T(8,128)S(1)}, f32[2,6,16,128]{3,2,1,0:T(8,128)S(1)}, u32[]{:S(2)}, u32[]{:S(2)}) collective-permute-start(f32[2,6,16,128]{3,2,1,0:T(8,128)S(1)} %get-tuple-element.7.own_ref), channel_id=1, source_target_pairs={{0,1},{1,2},{2,3},{3,0},{4,5},{5,6},{6,7},{7,4},{8,9},{9,10},{10,1... | collective-permute-start | bytes 294920 | tf_op jit(solution)/shard_map/ppermute | solution.py:309
  31.7 4.6 %collective-permute-start.5 = (f32[2,6,16,128]{3,2,1,0:T(8,128)S(1)}, f32[2,6,16,128]{3,2,1,0:T(8,128)S(1)}, u32[]{:S(2)}, u32[]{:S(2)}) collective-permute-start(f32[2,6,16,128]{3,2,1,0:T(8,128)S(1)} %get-tuple-element.7.own_ref), channel_id=1, source_target_pairs={{0,3},{1,0},{2,1},{3,2},{4,7},{5,4},{6,5},{7,6},{8,11},{9,8},{10,9... | collective-permute-start | bytes 294920 | tf_op jit(solution)/shard_map/ppermute | solution.py:309
